TPU v7x, 32 devices: a whole 2x2x4 slice. The times are simulated.
32 devices in a mesh: groups: 2 (over x), samp: 8 (over z, y), line: 2 (over core).
Axes of the slice: x: 2, y: 2, z: 4, core: 2. Of those that a mesh axis runs over, the one named last changes fastest.
Arguments:
- cube: float32 [7077888], P(('groups', 'samp', 'line')), parts along dimension 0, may hold values from -4000 to 4000
Outputs:
- details1: float32 [5308416], P(('groups', 'samp', 'line')), parts along dimension 0
- details2: float32 [1327104], P(('groups', 'samp', 'line')), parts along dimension 0
- details3: float32 [331776], P(('groups', 'samp', 'line')), parts along dimension 0
- approx: float32 [110592], P(('groups', 'samp', 'line')), parts along dimension 0
There are 2 independent parts, one for each index of `groups`. A program takes and returns all parts, laid end to end along the dimension named above; each array names one. Nothing has to cross between parts.
All inputs are finite; a program needn't handle non-finite values.
Results may differ from a plain program's by a relative error of at most 0.000088.
Values sent between devices are 32-bit elements; how exact they have to be, the bound alone decides.
A program may use at most 64 MiB of HBM per device.

v0:
```python
import functools
import jax
import jax.numpy as jnp
from jax import lax
from jax.experimental import pallas as pl
from jax.experimental.pallas import tpu as pltpu
from jax.sharding import PartitionSpec as P

MESH = pl.DeviceIdType.MESH
HIGH = lax.Precision.HIGHEST
LANES = 128


def blocks_of(bands):
    rows = [bands - start for start in range(0, bands, LANES)]
    offsets = [sum(rows[:i]) for i in range(len(rows))]
    return rows, offsets


def gram_kernel(samp, line, bands, pixels, x_ref, xc_ref, p_ref, xs, sums, sums_in, g, half_in,
                chunk_in, tot, s_send, s_recv, h_send, h_recv, c_send, c_recv, a_send, a_recv,
                b_send, b_recv):
    me, ln = lax.axis_index("samp"), lax.axis_index("line")
    devices = samp * line
    flat = me * line + ln
    packs = pixels // LANES
    padded = xs.shape[0]

    def peer(d):
        other = lax.rem(flat + d, devices)
        return {"samp": other // line, "line": lax.rem(other, line)}

    barrier = pltpu.get_barrier_semaphore()
    for d in range(1, devices):
        pl.semaphore_signal(barrier, inc=1, device_id=peer(d), device_id_type=MESH)
    if padded > bands:
        xs[bands:, :] = jnp.zeros((padded - bands, pixels), jnp.float32)
    for q in range(packs):
        xs[0:bands, q * LANES:(q + 1) * LANES] = x_ref[pl.ds(q, bands, stride=packs), :]
    sums[...] = lax.dot_general(jnp.ones((8, pixels), jnp.float32), xs[...], (((1,), (1,)), ((), ())),
                                precision=HIGH, preferred_element_type=jnp.float32)
    pl.semaphore_wait(barrier, devices - 1)
    copies = []
    for d in range(1, devices):
        copy = pltpu.make_async_remote_copy(sums, sums_in.at[d - 1], s_send.at[d - 1], s_recv.at[d - 1],
                                            device_id=peer(d), device_id_type=MESH)
        copy.start()
        copies.append(copy)
    for copy in copies:
        copy.wait()
    total = sums[...]
    for d in range(1, devices):
        total = total + sums_in[d - 1]
    mean = jnp.transpose(total / float(pixels * devices))[:, 0:1]
    xs[...] = xs[...] - mean
    xc_ref[...] = xs[0:bands, :]
    rows, offsets = blocks_of(bands)
    for q, (count, offset) in enumerate(zip(rows, offsets)):
        g[offset:offset + count, :] = lax.dot_general(
            xs[q * LANES:q * LANES + count, :], xs[q * LANES:(q + 1) * LANES, :],
            (((1,), (1,)), ((), ())), precision=HIGH, preferred_element_type=jnp.float32)
    used = offsets[-1] + rows[-1]
    if g.shape[0] > used:
        g[used:, :] = jnp.zeros((g.shape[0] - used, LANES), jnp.float32)
    half = g.shape[0] // line
    chunk = half // samp
    copies = []
    for d in range(1, line):
        other = lax.rem(ln + d, line)
        copy = pltpu.make_async_remote_copy(
            g.at[pl.ds(pl.multiple_of(other * half, 8), half)], half_in.at[d - 1], h_send.at[d - 1],
            h_recv.at[d - 1], device_id={"line": other}, device_id_type=MESH)
        copy.start()
        copies.append(copy)
    for copy in copies:
        copy.wait()
    mine = pl.ds(pl.multiple_of(ln * half, 8), half)
    value = g[mine, :]
    for d in range(1, line):
        value = value + half_in[d - 1]
    g[mine, :] = value
    copies = []
    for d in range(1, samp):
        other = lax.rem(me + d, samp)
        copy = pltpu.make_async_remote_copy(
            g.at[pl.ds(pl.multiple_of(ln * half + other * chunk, 8), chunk)], chunk_in.at[d - 1],
            c_send.at[d - 1], c_recv.at[d - 1], device_id={"samp": other}, device_id_type=MESH)
        copy.start()
        copies.append(copy)
    for copy in copies:
        copy.wait()
    own = pl.ds(pl.multiple_of(ln * half + me * chunk, 8), chunk)
    value = g[own, :]
    for d in range(1, samp):
        value = value + chunk_in[d - 1]
    tot[own, :] = value
    copies = []
    for d in range(1, samp):
        other = lax.rem(me + d, samp)
        copy = pltpu.make_async_remote_copy(tot.at[own], tot.at[own], a_send.at[d - 1], a_recv.at[d - 1],
                                            device_id={"samp": other}, device_id_type=MESH)
        copy.start()
        copies.append(copy)
    for copy in copies:
        copy.wait()
    copies = []
    for d in range(1, line):
        other = lax.rem(ln + d, line)
        copy = pltpu.make_async_remote_copy(tot.at[mine], tot.at[mine], b_send.at[d - 1], b_recv.at[d - 1],
                                            device_id={"line": other}, device_id_type=MESH)
        copy.start()
        copies.append(copy)
    for copy in copies:
        copy.wait()
    p_ref[...] = tot[...]


def gram_call(cube, bands, pixels):
    samp, line = lax.axis_size("samp"), lax.axis_size("line")
    devices = samp * line
    rows, offsets = blocks_of(bands)
    used = offsets[-1] + rows[-1]
    unit = 8 * devices
    total = -(-used // unit) * unit
    padded = -(-bands // LANES) * LANES
    f32 = jnp.float32
    sem = pltpu.SemaphoreType.DMA
    return pl.pallas_call(
        functools.partial(gram_kernel, samp, line, bands, pixels),
        out_shape=(jax.ShapeDtypeStruct((bands, pixels), f32), jax.ShapeDtypeStruct((total, LANES), f32)),
        in_specs=[pl.BlockSpec(memory_space=pltpu.VMEM)],
        out_specs=(pl.BlockSpec(memory_space=pltpu.VMEM), pl.BlockSpec(memory_space=pltpu.VMEM)),
        scratch_shapes=[
            pltpu.VMEM((padded, pixels), f32), pltpu.VMEM((8, padded), f32),
            pltpu.VMEM((devices - 1, 8, padded), f32), pltpu.VMEM((total, LANES), f32),
            pltpu.VMEM((line - 1, total // line, LANES), f32),
            pltpu.VMEM((samp - 1, total // devices, LANES), f32), pltpu.VMEM((total, LANES), f32),
            sem((devices - 1,)), sem((devices - 1,)), sem((line - 1,)), sem((line - 1,)),
            sem((samp - 1,)), sem((samp - 1,)), sem((samp - 1,)), sem((samp - 1,)),
            sem((line - 1,)), sem((line - 1,)),
        ],
        compiler_params=pltpu.CompilerParams(collective_id=0, has_side_effects=True),
    )(cube.reshape(-1, LANES))


def split3(value):
    first = value.astype(jnp.bfloat16).astype(jnp.float32)
    rest = value - first
    second = rest.astype(jnp.bfloat16).astype(jnp.float32)
    return first, second, rest - second


def inverse_kernel(bands, count, p_ref, w_ref, m):
    wide = m.shape[1]
    rows, offsets = blocks_of(bands)
    diag = lax.broadcasted_iota(jnp.int32, (LANES, LANES), 0) == lax.broadcasted_iota(
        jnp.int32, (LANES, LANES), 1)
    scale = 1.0 / float(count)
    trace = jnp.zeros((1, 1), jnp.float32)
    for q, offset in enumerate(offsets):
        size = min(LANES, rows[q])
        block = p_ref[offset:offset + size, :]
        kept = jnp.where(diag[:size], block, 0.0)
        trace = trace + jnp.sum(jnp.sum(kept, axis=0, keepdims=True), axis=1, keepdims=True)
    ridge = trace * scale * (0.01 / bands)
    for q, offset in enumerate(offsets):
        for b in range(q, len(rows)):
            size = min(LANES, rows[b])
            start = offset + (b - q) * LANES
            block = p_ref[start:start + size, :] * scale
            if b == q:
                low = jnp.where(diag[:size], block + ridge, block)
                m[q * LANES:q * LANES + size, q * LANES:(q + 1) * LANES] = low
            else:
                if size < LANES:
                    block = jnp.concatenate([block, jnp.zeros((LANES - size, LANES), jnp.float32)], axis=0)
                m[q * LANES:(q + 1) * LANES, b * LANES:(b + 1) * LANES] = jnp.transpose(block)
                m[b * LANES:b * LANES + size, q * LANES:(q + 1) * LANES] = block[:size]
    sub = lax.broadcasted_iota(jnp.int32, (8, LANES), 0)
    lane = lax.broadcasted_iota(jnp.int32, (8, LANES), 1)

    for c in range(len(rows)):
        top = c * LANES
        span = bands - top

        def step(j, carry):
            row = pl.multiple_of(top + 8 * j, 8)
            here = m[pl.ds(row, 8), top:top + LANES]
            small = pltpu.roll(here, lax.rem(LANES - 8 * j, LANES), 1)
            columns = [jnp.broadcast_to(small[:, b:b + 1], (8, LANES)) for b in range(8)]
            d = [[jnp.broadcast_to(columns[b][a:a + 1, :], (8, LANES)) if b <= a else None
                  for b in range(8)] for a in range(8)]
            low = [[None] * 8 for _ in range(8)]
            root = [None] * 8
            for b in range(8):
                root[b] = lax.rsqrt(d[b][b])
                for a in range(b + 1, 8):
                    low[a][b] = d[a][b] * root[b]
                for a in range(b + 1, 8):
                    for e in range(b + 1, a + 1):
                        d[a][e] = d[a][e] - low[a][b] * low[e][b]
            inv = [[None] * 8 for _ in range(8)]
            for b in range(8):
                inv[b][b] = root[b]
                for a in range(b + 1, 8):
                    acc = low[a][b] * inv[b][b]
                    for e in range(b + 1, a):
                        acc = acc + low[a][e] * inv[e][b]
                    inv[a][b] = -(acc * root[a])
            wcol = []
            for b in range(8):
                col = jnp.where(sub == b, inv[b][b], 0.0)
                for a in range(b + 1, 8):
                    col = jnp.where(sub == a, inv[a][b], col)
                wcol.append(col)
            tiles = []
            for t in range(wide // LANES):
                acc = None
                panel = m[pl.ds(row, 8), t * LANES:(t + 1) * LANES]
                for b in range(8):
                    term = wcol[b] * panel[b:b + 1, :]
                    acc = term if acc is None else acc + term
                if t == c:
                    for b in range(8):
                        acc = jnp.where(lane == 8 * j + b, wcol[b], acc)
                tiles.append(acc)
            r = jnp.concatenate(tiles, axis=1)
            m[pl.ds(row, 8), :] = r
            one, two, three = split3(r)
            right = jnp.concatenate([one, two, three, one, two, one], axis=0)
            cols = lax.broadcasted_iota(jnp.int32, (8, wide), 1)
            keep = (cols >= row + 8).astype(jnp.float32)
            l1, l2, l3 = one * keep, two * keep, three * keep
            left = jnp.concatenate([l1, l1, l1, l2, l2, l3], axis=0)[:, top:]
            update = lax.dot_general(
                jnp.transpose(left).astype(jnp.bfloat16), right.astype(jnp.bfloat16),
                (((1,), (0,)), ((), ())), preferred_element_type=jnp.float32)
            for t in range(wide // LANES):
                part = slice(t * LANES, (t + 1) * LANES)
                old = m[top:bands, part]
                if t == c:
                    line_ids = lax.broadcasted_iota(jnp.int32, (span, LANES), 0)
                    lane_ids = lax.broadcasted_iota(jnp.int32, (span, LANES), 1)
                    inside = (lane_ids >= 8 * j) & (lane_ids < 8 * j + 8) & (line_ids >= 8 * j + 8)
                    old = jnp.where(inside, 0.0, old)
                m[top:bands, part] = old - update[:span, part]
            return carry

        lax.fori_loop(0, min(LANES, span) // 8, step, 0)
    keep = lax.broadcasted_iota(jnp.int32, (bands, wide), 1) <= lax.broadcasted_iota(
        jnp.int32, (bands, wide), 0)
    w_ref[...] = jnp.where(keep, m[...], 0.0)[:, :bands]


def inverse_call(packed, bands, count):
    wide = -(-bands // LANES) * LANES
    return pl.pallas_call(
        functools.partial(inverse_kernel, bands, count),
        out_shape=jax.ShapeDtypeStruct((bands, bands), jnp.float32),
        in_specs=[pl.BlockSpec(memory_space=pltpu.VMEM)],
        out_specs=pl.BlockSpec(memory_space=pltpu.VMEM),
        scratch_shapes=[pltpu.VMEM((bands, wide), jnp.float32)],
    )(packed)

BANDS = 432
LD = 32
SD = 16


alpha_lift = -1.586134342059924
beta_lift = -0.052980118572961
gamma_lift = 0.882911075530934
delta_lift = 0.443506852043971
scale_lift = 1.230174104914001


def passed_along(array, axis, by):
    count = lax.axis_size(axis)
    pairs = [(i, i + by) for i in range(count) if 0 <= i + by < count]
    return lax.ppermute(array, axis, pairs)


def with_halo(block, sides, width):
    for axis, dim in sides:
        count = lax.axis_size(axis)
        forward = [(i, i + 1) for i in range(count - 1)]
        backward = [(target, source) for source, target in forward]
        low = lax.ppermute(
            lax.slice_in_dim(block, block.shape[dim] - width, None, axis=dim), axis, forward
        )
        high = lax.ppermute(lax.slice_in_dim(block, 0, width, axis=dim), axis, backward)
        block = jnp.concatenate([low, block, high], axis=dim)
    return block


def lines_next(edge):
    return passed_along(edge, "line", -1)


def lines_prev(edge):
    return passed_along(edge, "line", 1)


def split_pairs(values, axis):
    length = values.shape[axis]
    return (
        lax.slice_in_dim(values, 0, length, 2, axis),
        lax.slice_in_dim(values, 1, length, 2, axis),
    )


def lift_steps(values, axis, fetch_next, fetch_prev, at_first, at_last):
    evens, odds = split_pairs(values, axis)
    half = evens.shape[axis]
    for weight_odd, weight_even in ((alpha_lift, beta_lift), (gamma_lift, delta_lift)):
        own_last = lax.slice_in_dim(evens, half - 1, half, 1, axis)
        arrived = fetch_next(lax.slice_in_dim(evens, 0, 1, 1, axis))
        beyond = jnp.where(at_last, own_last, arrived)
        following = jnp.concatenate([lax.slice_in_dim(evens, 1, half, 1, axis), beyond], axis)
        odds = odds + weight_odd * (evens + following)
        own_first = lax.slice_in_dim(odds, 0, 1, 1, axis)
        received = fetch_prev(lax.slice_in_dim(odds, half - 1, half, 1, axis))
        before = jnp.where(at_first, own_first, received)
        preceding = jnp.concatenate([before, lax.slice_in_dim(odds, 0, half - 1, 1, axis)], axis)
        evens = evens + weight_even * (preceding + odds)
    return (evens / scale_lift, odds * scale_lift)


def lift_rims(values, at_first, at_last):
    length = values.shape[2]
    widened = with_halo(values, (("samp", 2),), 4)
    from_left = widened[:, :, :4]
    from_right = widened[:, :, length + 4 :]
    with_right = jnp.concatenate([values, from_right], 2)
    with_left = jnp.concatenate([from_left, values], 2)
    left_mirror = jnp.flip(with_right[:, :, 1:5], axis=2)
    right_mirror = jnp.flip(with_left[:, :, length - 1 : length + 3], axis=2)
    left_rim = jnp.where(at_first, left_mirror, from_left)
    right_rim = jnp.where(at_last, right_mirror, from_right)
    extended = jnp.concatenate([left_rim, values, right_rim], 2)
    evens, odds = split_pairs(extended, 2)
    odds = odds[..., :-1] + alpha_lift * (evens[..., :-1] + evens[..., 1:])
    evens = evens[..., 1:-1] + beta_lift * (odds[..., :-1] + odds[..., 1:])
    odds = odds[..., 1:-1] + gamma_lift * (evens[..., :-1] + evens[..., 1:])
    evens = evens[..., 1:-1] + delta_lift * (odds[..., :-1] + odds[..., 1:])
    return (evens / scale_lift, odds[..., 1:] * scale_lift)


def local(cube):
    band_count = BANDS
    line_count = LD
    samples = SD
    tile = cube.reshape(band_count, line_count, samples)
    pixels = line_count * samples
    devices = lax.axis_size("samp") * lax.axis_size("line")
    centered, packed = gram_call(cube, band_count, pixels)
    whitener = inverse_call(packed, band_count, pixels * devices)
    components = jnp.dot(
        whitener, centered, precision=lax.Precision.HIGHEST, preferred_element_type=jnp.float32
    ).reshape(tile.shape)
    samp_first = lax.axis_index("samp") == 0
    samp_last = lax.axis_index("samp") == lax.axis_size("samp") - 1
    line_first = lax.axis_index("line") == 0
    line_last = lax.axis_index("line") == lax.axis_size("line") - 1

    def decompose(values):
        low_s, high_s = lift_rims(values, samp_first, samp_last)
        joined = jnp.concatenate([low_s, high_s], 2)
        low_l, high_l = lift_steps(joined, 1, lines_next, lines_prev, line_first, line_last)
        middle = low_s.shape[2]
        details = jnp.stack([high_l[:, :, :middle], low_l[:, :, middle:], high_l[:, :, middle:]])
        return (low_l[:, :, :middle], details)

    approx1, details1 = decompose(components)
    approx2, details2 = decompose(approx1)
    approx3, details3 = decompose(approx2)
    return (details1.reshape(-1), details2.reshape(-1), details3.reshape(-1), approx3.reshape(-1))


def solution(mesh):
    in_specs = (P(("groups", "samp", "line")),)
    out_specs = (
        P(("groups", "samp", "line")),
        P(("groups", "samp", "line")),
        P(("groups", "samp", "line")),
        P(("groups", "samp", "line")),
    )
    return jax.shard_map(local, mesh=mesh, in_specs=in_specs, out_specs=out_specs, check_vma=False)
```

profile of v0, /device:TPU:0, one launch (start us, length us, event | category | flops | bytes accessed | tf_op | source)
XLA Modules:
  0.0 182.7 jit_solution(10649554983852323663)
XLA Ops:
  0.6 34.2 %shard_map.46 = (f32[432,512]{1,0:T(8,128)}, f32[1024,128]{1,0:T(8,128)}) custom-call(f32[1728,128]{1,0:T(8,128)} %bitcast.47), custom_call_target="tpu_custom_call" | custom-call | tf_op jit(solution)/shard_map/pallas_call | solution.py:128
  34.9 32.5 %shard_map.47 = f32[432,432]{1,0:T(8,128)} custom-call(f32[1024,128]{1,0:T(8,128)} %get-tuple-element.6.p_ref), custom_call_target="tpu_custom_call" | custom-call | tf_op jit(solution)/shard_map/pallas_call | solution.py:257
  67.3 3.1 %fusion.62 = f32[432,512]{0,1:T(8,128)S(1)} fusion(f32[432,432]{1,0:T(8,128)} %shard_map.47, f32[432,512]{1,0:T(8,128)S(1)} %copy-done), kind=kOutput, calls=%fused_computation.127 | convolution fusion | flops 1146617856 | bytes 2515968 | tf_op jit(solution)/shard_map/dot_general | solution.py:358
  70.6 3.8 %collective-permute-start = (f32[432,32,4]{0,2,1:T(4,128)S(1)}, f32[432,32,4]{0,2,1:T(4,128)S(1)}, u32[]{:S(2)}, u32[]{:S(2)}) collective-permute-start(f32[432,32,4]{0,2,1:T(4,128)S(1)} %get-tuple-element.16), channel_id=1, source_target_pairs={{0,2},{2,4},{4,6},{6,8},{8,10},{10,12},{12,14},{1,3},{3,5},{5,7},{... | collective-permute-start | bytes 663560 | tf_op jit(solution)/shard_map/ppermute | solution.py:288
  74.4 1.3 collective-permute-start.1
  75.7 0.4 rev.22
  76.1 0.4 rev.21
  76.6 9.5 %collective-permute-done = f32[432,32,4]{0,2,1:T(4,128)S(1)} collective-permute-done((f32[432,32,4]{0,2,1:T(4,128)S(1)}, f32[432,32,4]{0,2,1:T(4,128)S(1)}, u32[]{:S(2)}, u32[]{:S(2)}) %collective-permute-start) | collective-permute-done | bytes 221216 | tf_op jit(solution)/shard_map/ppermute | solution.py:288
  86.5 0.5 slice.329
  86.9 2.8 %slice.331 = f32[432,32,12]{0,2,1:T(8,128)} slice(f32[432,32,24]{0,2,1:T(8,128)S(1)} %pad_maximum_fusion), slice={[0:432:1], [0:32:1], [1:24:2]} | slice | bytes 1327104 | tf_op jit(solution)/shard_map/slice | solution.py:308
  89.8 1.5 fusion.5
  92.4 1.3 collective-permute-start.2
  93.7 1.8 collective-permute-done.2
  95.7 2.1 %collective-permute-start.3 = (f32[432,1,16]{0,2,1:T(8,128)S(1)}, f32[432,1,16]{0,2,1:T(8,128)S(1)}, u32[]{:S(2)}, u32[]{:S(2)}) collective-permute-start(f32[432,1,16]{0,2,1:T(8,128)S(1)} %slice.451), channel_id=1, source_target_pairs={{0,1},{2,3},{4,5},{6,7},{8,9},{10,11},{12,13},{14,15},{16,17},{18,... | collective-permute-start | bytes 82952 | tf_op jit(solution)/shard_map/ppermute | solution.py:280
  97.8 0.8 collective-permute-done.3
  98.8 1.3 collective-permute-start.4
  100.1 1.8 collective-permute-done.4
  102.1 2.1 %collective-permute-start.5 = (f32[432,1,16]{0,2,1:T(8,128)S(1)}, f32[432,1,16]{0,2,1:T(8,128)S(1)}, u32[]{:S(2)}, u32[]{:S(2)}) collective-permute-start(f32[432,1,16]{0,2,1:T(8,128)S(1)} %slice.458), channel_id=1, source_target_pairs={{0,1},{2,3},{4,5},{6,7},{8,9},{10,11},{12,13},{14,15},{16,17},{18,... | collective-permute-start | bytes 82952 | tf_op jit(solution)/shard_map/ppermute | solution.py:280
  104.2 0.8 collective-permute-done.5
  105.3 4.4 %collective-permute-start.6 = (f32[432,16,4]{0,2,1:T(4,128)S(1)}, f32[432,16,4]{0,2,1:T(4,128)S(1)}, u32[]{:S(2)}, u32[]{:S(2)}) collective-permute-start(f32[432,16,4]{0,2,1:T(4,128)S(1)} %get-tuple-element.20), channel_id=1, source_target_pairs={{0,2},{2,4},{4,6},{6,8},{8,10},{10,12},{12,14},{1,3},{3,5},{5,7},{... | collective-permute-start | bytes 331784 | tf_op jit(solution)/shard_map/ppermute | solution.py:288
  110.3 1.3 collective-permute-start.7
  111.6 1.3 collective-permute-done.6
  113.0 5.4 %collective-permute-done.7 = f32[432,16,4]{0,2,1:T(4,128)S(1)} collective-permute-done((f32[432,16,4]{0,2,1:T(4,128)S(1)}, f32[432,16,4]{0,2,1:T(4,128)S(1)}, u32[]{:S(2)}, u32[]{:S(2)}) %collective-permute-start.7) | collective-permute-done | bytes 110624 | tf_op jit(solution)/shard_map/ppermute | solution.py:291
  119.6 1.3 collective-permute-start.8
  120.9 1.8 collective-permute-done.8
  122.7 2.1 %collective-permute-start.9 = (f32[432,1,8]{0,2,1:T(8,128)S(1)}, f32[432,1,8]{0,2,1:T(8,128)S(1)}, u32[]{:S(2)}, u32[]{:S(2)}) collective-permute-start(f32[432,1,8]{0,2,1:T(8,128)S(1)} %slice.483), channel_id=1, source_target_pairs={{0,1},{2,3},{4,5},{6,7},{8,9},{10,11},{12,13},{14,15},{16,17},{18,... | collective-permute-start | bytes 41480 | tf_op jit(solution)/shard_map/ppermute | solution.py:280
  124.8 0.8 collective-permute-done.9
  125.7 1.3 collective-permute-start.10
  127.0 1.8 collective-permute-done.10
  128.8 2.1 %collective-permute-start.11 = (f32[432,1,8]{0,2,1:T(8,128)S(1)}, f32[432,1,8]{0,2,1:T(8,128)S(1)}, u32[]{:S(2)}, u32[]{:S(2)}) collective-permute-start(f32[432,1,8]{0,2,1:T(8,128)S(1)} %slice.490), channel_id=1, source_target_pairs={{0,1},{2,3},{4,5},{6,7},{8,9},{10,11},{12,13},{14,15},{16,17},{18,... | collective-permute-start | bytes 41480 | tf_op jit(solution)/shard_map/ppermute | solution.py:280
  130.9 0.8 collective-permute-done.11
  131.8 1.3 collective-permute-start.12
  133.1 5.3 %collective-permute-start.13 = (f32[432,8,4]{0,2,1:T(4,128)S(1)}, f32[432,8,4]{0,2,1:T(4,128)S(1)}, u32[]{:S(2)}, u32[]{:S(2)}) collective-permute-start(f32[432,8,4]{0,2,1:T(4,128)S(1)} %get-tuple-element.30), channel_id=1, source_target_pairs={{0,2},{2,4},{4,6},{6,8},{8,10},{10,12},{12,14},{1,3},{3,5},{5,7},{... | collective-permute-start | bytes 165896 | tf_op jit(solution)/shard_map/ppermute | solution.py:288
  138.5 0.4 collective-permute-done.12
  139.2 1.3 collective-permute-done.13
  141.3 1.3 collective-permute-start.14
  142.7 6.1 %copy.6 = f32[3,432,16,8]{3,2,1,0:T(8,128)} copy(f32[3,432,16,8]{1,3,2,0:T(8,128)S(1)} %pad_maximum_fusion.2) | data formatting | bytes 1327104 | tf_op jit(solution)/shard_map/stack | solution.py:371
  148.8 8.6 %reshape.28 = f32[165888]{0:T(1024)} reshape(f32[3,432,16,8]{3,2,1,0:T(8,128)} %copy.6) | data formatting | bytes 1327104 | tf_op jit(solution)/shard_map/reshape | solution.py:377
  157.4 3.0 %collective-permute-start.15 = (f32[432,1,4]{0,2,1:T(4,128)S(1)}, f32[432,1,4]{0,2,1:T(4,128)S(1)}, u32[]{:S(2)}, u32[]{:S(2)}) collective-permute-start(f32[432,1,4]{0,2,1:T(4,128)S(1)} %slice.511), channel_id=1, source_target_pairs={{0,1},{2,3},{4,5},{6,7},{8,9},{10,11},{12,13},{14,15},{16,17},{18,... | collective-permute-start | bytes 20744 | tf_op jit(solution)/shard_map/ppermute | solution.py:280
  160.5 0.8 collective-permute-done.15
  161.3 1.3 collective-permute-start.16
  162.7 3.7 %copy.7 = f32[3,432,8,4]{3,2,1,0:T(8,128)} copy(f32[3,432,8,4]{1,3,2,0:T(4,128)S(1)} %pad_maximum_fusion.6) | data formatting | bytes 331776 | tf_op jit(solution)/shard_map/stack | solution.py:371
  166.3 6.3 %reshape.29 = f32[41472]{0:T(1024)} reshape(f32[3,432,8,4]{3,2,1,0:T(8,128)} %copy.7) | data formatting | bytes 331776 | tf_op jit(solution)/shard_map/reshape | solution.py:377
  172.7 3.0 %collective-permute-start.17 = (f32[432,1,4]{0,2,1:T(4,128)S(1)}, f32[432,1,4]{0,2,1:T(4,128)S(1)}, u32[]{:S(2)}, u32[]{:S(2)}) collective-permute-start(f32[432,1,4]{0,2,1:T(4,128)S(1)} %slice.518), channel_id=1, source_target_pairs={{0,1},{2,3},{4,5},{6,7},{8,9},{10,11},{12,13},{14,15},{16,17},{18,... | collective-permute-start | bytes 20744 | tf_op jit(solution)/shard_map/ppermute | solution.py:280
  175.7 0.8 collective-permute-done.17
  176.9 1.4 reshape.31
  178.3 1.2 copy.8
  179.5 3.2 %reshape.30 = f32[10368]{0:T(1024)} reshape(f32[3,432,4,2]{3,2,1,0:T(4,128)S(1)} %copy.8) | data formatting | bytes 82944 | tf_op jit(solution)/shard_map/reshape | solution.py:377
  (100 shorter events, 6.3 us)
Async XLA Ops:
  34.9 32.5 %copy-start = (f32[432,512]{1,0:T(8,128)S(1)}, f32[432,512]{1,0:T(8,128)}, u32[]{:S(2)}) copy-start(f32[432,512]{1,0:T(8,128)} %get-tuple-element.7) | copy-start | bytes 2654212
  70.6 15.5 %collective-permute-start = (f32[432,32,4]{0,2,1:T(4,128)S(1)}, f32[432,32,4]{0,2,1:T(4,128)S(1)}, u32[]{:S(2)}, u32[]{:S(2)}) collective-permute-start(f32[432,32,4]{0,2,1:T(4,128)S(1)} %get-tuple-element.16), channel_id=1, source_target_pairs={{0,2},{2,4},{4,6},{6,8},{8,10},{10,12},{12,14},{1,3},{3,5},{5,7},{... | collective-permute-start | bytes 663560 | tf_op jit(solution)/shard_map/ppermute | solution.py:288
  74.4 11.7 %collective-permute-start.1 = (f32[432,32,4]{0,2,1:T(4,128)S(1)}, f32[432,32,4]{0,2,1:T(4,128)S(1)}, u32[]{:S(2)}, u32[]{:S(2)}) collective-permute-start(f32[432,32,4]{0,2,1:T(4,128)S(1)} %get-tuple-element.17), channel_id=1, source_target_pairs={{2,0},{4,2},{6,4},{8,6},{10,8},{12,10},{14,12},{3,1},{5,3},{7,5},{... | collective-permute-start | bytes 663560 | tf_op jit(solution)/shard_map/ppermute | solution.py:291
  92.4 3.1 %collective-permute-start.2 = (f32[432,1,16]{0,2,1:T(8,128)S(1)}, f32[432,1,16]{0,2,1:T(8,128)S(1)}, u32[]{:S(2)}, u32[]{:S(2)}) collective-permute-start(f32[432,1,16]{0,2,1:T(8,128)S(1)} %slice.449), channel_id=1, source_target_pairs={{1,0},{3,2},{5,4},{7,6},{9,8},{11,10},{13,12},{15,14},{17,16},{19,... | collective-permute-start | bytes 82952 | tf_op jit(solution)/shard_map/ppermute | solution.py:280
  95.7 2.9 %collective-permute-start.3 = (f32[432,1,16]{0,2,1:T(8,128)S(1)}, f32[432,1,16]{0,2,1:T(8,128)S(1)}, u32[]{:S(2)}, u32[]{:S(2)}) collective-permute-start(f32[432,1,16]{0,2,1:T(8,128)S(1)} %slice.451), channel_id=1, source_target_pairs={{0,1},{2,3},{4,5},{6,7},{8,9},{10,11},{12,13},{14,15},{16,17},{18,... | collective-permute-start | bytes 82952 | tf_op jit(solution)/shard_map/ppermute | solution.py:280
  98.8 3.1 %collective-permute-start.4 = (f32[432,1,16]{0,2,1:T(8,128)S(1)}, f32[432,1,16]{0,2,1:T(8,128)S(1)}, u32[]{:S(2)}, u32[]{:S(2)}) collective-permute-start(f32[432,1,16]{0,2,1:T(8,128)S(1)} %slice.455), channel_id=1, source_target_pairs={{1,0},{3,2},{5,4},{7,6},{9,8},{11,10},{13,12},{15,14},{17,16},{19,... | collective-permute-start | bytes 82952 | tf_op jit(solution)/shard_map/ppermute | solution.py:280
  102.1 2.9 %collective-permute-start.5 = (f32[432,1,16]{0,2,1:T(8,128)S(1)}, f32[432,1,16]{0,2,1:T(8,128)S(1)}, u32[]{:S(2)}, u32[]{:S(2)}) collective-permute-start(f32[432,1,16]{0,2,1:T(8,128)S(1)} %slice.458), channel_id=1, source_target_pairs={{0,1},{2,3},{4,5},{6,7},{8,9},{10,11},{12,13},{14,15},{16,17},{18,... | collective-permute-start | bytes 82952 | tf_op jit(solution)/shard_map/ppermute | solution.py:280
  105.3 7.6 %collective-permute-start.6 = (f32[432,16,4]{0,2,1:T(4,128)S(1)}, f32[432,16,4]{0,2,1:T(4,128)S(1)}, u32[]{:S(2)}, u32[]{:S(2)}) collective-permute-start(f32[432,16,4]{0,2,1:T(4,128)S(1)} %get-tuple-element.20), channel_id=1, source_target_pairs={{0,2},{2,4},{4,6},{6,8},{8,10},{10,12},{12,14},{1,3},{3,5},{5,7},{... | collective-permute-start | bytes 331784 | tf_op jit(solution)/shard_map/ppermute | solution.py:288
  110.3 8.1 %collective-permute-start.7 = (f32[432,16,4]{0,2,1:T(4,128)S(1)}, f32[432,16,4]{0,2,1:T(4,128)S(1)}, u32[]{:S(2)}, u32[]{:S(2)}) collective-permute-start(f32[432,16,4]{0,2,1:T(4,128)S(1)} %get-tuple-element.21), channel_id=1, source_target_pairs={{2,0},{4,2},{6,4},{8,6},{10,8},{12,10},{14,12},{3,1},{5,3},{7,5},{... | collective-permute-start | bytes 331784 | tf_op jit(solution)/shard_map/ppermute | solution.py:291
  119.6 3.1 %collective-permute-start.8 = (f32[432,1,8]{0,2,1:T(8,128)S(1)}, f32[432,1,8]{0,2,1:T(8,128)S(1)}, u32[]{:S(2)}, u32[]{:S(2)}) collective-permute-start(f32[432,1,8]{0,2,1:T(8,128)S(1)} %slice.481), channel_id=1, source_target_pairs={{1,0},{3,2},{5,4},{7,6},{9,8},{11,10},{13,12},{15,14},{17,16},{19,... | collective-permute-start | bytes 41480 | tf_op jit(solution)/shard_map/ppermute | solution.py:280
  122.7 2.9 %collective-permute-start.9 = (f32[432,1,8]{0,2,1:T(8,128)S(1)}, f32[432,1,8]{0,2,1:T(8,128)S(1)}, u32[]{:S(2)}, u32[]{:S(2)}) collective-permute-start(f32[432,1,8]{0,2,1:T(8,128)S(1)} %slice.483), channel_id=1, source_target_pairs={{0,1},{2,3},{4,5},{6,7},{8,9},{10,11},{12,13},{14,15},{16,17},{18,... | collective-permute-start | bytes 41480 | tf_op jit(solution)/shard_map/ppermute | solution.py:280
  125.7 3.1 %collective-permute-start.10 = (f32[432,1,8]{0,2,1:T(8,128)S(1)}, f32[432,1,8]{0,2,1:T(8,128)S(1)}, u32[]{:S(2)}, u32[]{:S(2)}) collective-permute-start(f32[432,1,8]{0,2,1:T(8,128)S(1)} %slice.487), channel_id=1, source_target_pairs={{1,0},{3,2},{5,4},{7,6},{9,8},{11,10},{13,12},{15,14},{17,16},{19,... | collective-permute-start | bytes 41480 | tf_op jit(solution)/shard_map/ppermute | solution.py:280
  128.8 2.9 %collective-permute-start.11 = (f32[432,1,8]{0,2,1:T(8,128)S(1)}, f32[432,1,8]{0,2,1:T(8,128)S(1)}, u32[]{:S(2)}, u32[]{:S(2)}) collective-permute-start(f32[432,1,8]{0,2,1:T(8,128)S(1)} %slice.490), channel_id=1, source_target_pairs={{0,1},{2,3},{4,5},{6,7},{8,9},{10,11},{12,13},{14,15},{16,17},{18,... | collective-permute-start | bytes 41480 | tf_op jit(solution)/shard_map/ppermute | solution.py:280
  131.8 7.1 %collective-permute-start.12 = (f32[432,8,4]{0,2,1:T(4,128)S(1)}, f32[432,8,4]{0,2,1:T(4,128)S(1)}, u32[]{:S(2)}, u32[]{:S(2)}) collective-permute-start(f32[432,8,4]{0,2,1:T(4,128)S(1)} %get-tuple-element.30), channel_id=1, source_target_pairs={{2,0},{4,2},{6,4},{8,6},{10,8},{12,10},{14,12},{3,1},{5,3},{7,5},{... | collective-permute-start | bytes 165896 | tf_op jit(solution)/shard_map/ppermute | solution.py:291
  133.1 7.3 %collective-permute-start.13 = (f32[432,8,4]{0,2,1:T(4,128)S(1)}, f32[432,8,4]{0,2,1:T(4,128)S(1)}, u32[]{:S(2)}, u32[]{:S(2)}) collective-permute-start(f32[432,8,4]{0,2,1:T(4,128)S(1)} %get-tuple-element.30), channel_id=1, source_target_pairs={{0,2},{2,4},{4,6},{6,8},{8,10},{10,12},{12,14},{1,3},{3,5},{5,7},{... | collective-permute-start | bytes 165896 | tf_op jit(solution)/shard_map/ppermute | solution.py:288
  141.3 16.1 %collective-permute-start.14 = (f32[432,1,4]{0,2,1:T(4,128)S(1)}, f32[432,1,4]{0,2,1:T(4,128)S(1)}, u32[]{:S(2)}, u32[]{:S(2)}) collective-permute-start(f32[432,1,4]{0,2,1:T(4,128)S(1)} %slice.509), channel_id=1, source_target_pairs={{1,0},{3,2},{5,4},{7,6},{9,8},{11,10},{13,12},{15,14},{17,16},{19,... | collective-permute-start | bytes 20744 | tf_op jit(solution)/shard_map/ppermute | solution.py:280
  157.4 3.8 %collective-permute-start.15 = (f32[432,1,4]{0,2,1:T(4,128)S(1)}, f32[432,1,4]{0,2,1:T(4,128)S(1)}, u32[]{:S(2)}, u32[]{:S(2)}) collective-permute-start(f32[432,1,4]{0,2,1:T(4,128)S(1)} %slice.511), channel_id=1, source_target_pairs={{0,1},{2,3},{4,5},{6,7},{8,9},{10,11},{12,13},{14,15},{16,17},{18,... | collective-permute-start | bytes 20744 | tf_op jit(solution)/shard_map/ppermute | solution.py:280
  161.3 11.3 %collective-permute-start.16 = (f32[432,1,4]{0,2,1:T(4,128)S(1)}, f32[432,1,4]{0,2,1:T(4,128)S(1)}, u32[]{:S(2)}, u32[]{:S(2)}) collective-permute-start(f32[432,1,4]{0,2,1:T(4,128)S(1)} %slice.515), channel_id=1, source_target_pairs={{1,0},{3,2},{5,4},{7,6},{9,8},{11,10},{13,12},{15,14},{17,16},{19,... | collective-permute-start | bytes 20744 | tf_op jit(solution)/shard_map/ppermute | solution.py:280
  172.7 3.8 %collective-permute-start.17 = (f32[432,1,4]{0,2,1:T(4,128)S(1)}, f32[432,1,4]{0,2,1:T(4,128)S(1)}, u32[]{:S(2)}, u32[]{:S(2)}) collective-permute-start(f32[432,1,4]{0,2,1:T(4,128)S(1)} %slice.518), channel_id=1, source_target_pairs={{0,1},{2,3},{4,5},{6,7},{8,9},{10,11},{12,13},{14,15},{16,17},{18,... | collective-permute-start | bytes 20744 | tf_op jit(solution)/shard_map/ppermute | solution.py:280
where the time goes:
time: 185 us; the launch traced here: 183 us
  Pallas kernels  66.7 us (36%)
  starting transfers between devices  39.4 us (21%)
  local copies, waits for them, and re-layouts  37.4 us (20%)
  waiting for transfers between devices  29.8 us (16%)
  other arithmetic  4.89 us (3%)
  matrix products  3.08 us (2%)
    pallas_call x1, Pallas kernels, gram_call(): pl.pallas_call(functools.partial(gram_kernel, samp, line, bands, pixels),...  34.2 us
    pallas_call x1, Pallas kernels, inverse_call(): pl.pallas_call(functools.partial(inverse_kernel, bands, count), out_shape...  32.5 us
    ppermute x12, starting transfers between devices, passed_along(): return lax.ppermute(array, axis, pairs)  22.1 us
    ppermute x3, starting transfers between devices, with_halo(): lax.ppermute(lax.slice_in_dim(block, block.shape[dim] - width, None, axis...  13.5 us
    ppermute x3, waiting for transfers between devices, with_halo(): lax.ppermute(lax.slice_in_dim(block, block.shape[dim] - width, None, axis...  12.2 us
    ppermute x12, waiting for transfers between devices, passed_along(): return lax.ppermute(array, axis, pairs)  11.8 us
    another operation x6, local copies, waits for them, and re-layouts, decompose(): jnp.stack([high_l[:, :, :middle], low_l[:, :, middle:], high_l[:, :, midd...  11 us
    reshape x1, local copies, waits for them, and re-layouts, local(): details1.reshape(-1)  8.63 us
  transfers between devices with their start and end apart: 18, of which 15 were waited for; matrix products, arithmetic and copies ran while one was open for 15% of the time, Pallas kernels for 0%

commit v1 on v0

--- a/solution.py
+++ b/solution.py
@@ -6,6 +6,10 @@
 from jax.experimental.pallas import tpu as pltpu
 from jax.sharding import PartitionSpec as P
 
+BANDS = 432
+LD = 32
+SD = 16
+
 MESH = pl.DeviceIdType.MESH
 HIGH = lax.Precision.HIGHEST
 LANES = 128
@@ -17,11 +21,66 @@
     return rows, offsets
 
 
-def gram_kernel(samp, line, bands, pixels, x_ref, xc_ref, p_ref, xs, sums, sums_in, g, half_in,
+alpha_lift = -1.586134342059924
+beta_lift = -0.052980118572961
+gamma_lift = 0.882911075530934
+delta_lift = 0.443506852043971
+scale_lift = 1.230174104914001
+RIM = 4
+
+
+def lift_list(values):
+    evens, odds = values[0::2], values[1::2]
+    odds = [o + alpha_lift * (e + f) for o, e, f in zip(odds[:-1], evens[:-1], evens[1:])]
+    evens = [e + beta_lift * (o + q) for e, o, q in zip(evens[1:-1], odds[:-1], odds[1:])]
+    odds = [o + gamma_lift * (e + f) for o, e, f in zip(odds[1:-1], evens[:-1], evens[1:])]
+    evens = [e + delta_lift * (o + q) for e, o, q in zip(evens[1:-1], odds[:-1], odds[1:])]
+    return [e * (1.0 / scale_lift) for e in evens], [o * scale_lift for o in odds[1:]]
+
+
+def lift_lines(src, halo, dst, lines, width, ln):
+    half = lines // 2
+    for t in range(src.shape[0]):
+        own = [src[t, i * width:(i + 1) * width] for i in range(lines)]
+        got = [halo[t, i * width:(i + 1) * width] for i in range(RIM)]
+        before = [jnp.where(ln == 0, own[RIM - i], got[i]) for i in range(RIM)]
+        after = [jnp.where(ln == 0, got[i], own[lines - 2 - i]) for i in range(RIM)]
+        low, high = lift_list(before + own + after)
+        for i in range(half):
+            dst[t, i * width:(i + 1) * width] = low[i]
+            dst[t, (half + i) * width:(half + i + 1) * width] = high[i]
+
+
+def rims(z, lines, width, left, right):
+    for t in range(z.shape[0]):
+        for c in range(RIM):
+            left[t, c * lines:(c + 1) * lines] = z[t, pl.ds(c, lines, stride=width), :]
+            right[t, c * lines:(c + 1) * lines] = z[t, pl.ds(width - RIM + c, lines, stride=width), :]
+
+
+def lift_samples(z, from_left, from_right, lines, width, first, last, dests):
+    half = lines // 2
+    for t in range(z.shape[0]):
+        own = [z[t, pl.ds(s, lines, stride=width), :] for s in range(width)]
+        left = [from_left[t, c * lines:(c + 1) * lines] for c in range(RIM)]
+        right = [from_right[t, c * lines:(c + 1) * lines] for c in range(RIM)]
+        whole = left + own + right
+        before = [jnp.where(first, whole[2 * RIM - i], left[i]) for i in range(RIM)]
+        after = [jnp.where(last, whole[RIM + width - 2 - i], right[i]) for i in range(RIM)]
+        low, high = lift_list(before + own + after)
+        for i in range(width // 2):
+            for (ref, base), value in zip(dests, (low[i][:half], low[i][half:], high[i][:half], high[i][half:])):
+                ref[t, pl.ds(base + i, half, stride=width // 2), :] = value
+
+
+def gram_kernel(samp, line, bands, lines, width, x_ref, t_ref, p_ref, v1, v2, v3, z1, z2, z3, n1, n2, n3, el1, er1, el2, er2, el3, er3, fl1, fr1, fl2, fr2, fl3, fr3,
+                l_send, l_recv, r_send, r_recv, xs, sums, sums_in, g, half_in,
                 chunk_in, tot, s_send, s_recv, h_send, h_recv, c_send, c_recv, a_send, a_recv,
                 b_send, b_recv):
     me, ln = lax.axis_index("samp"), lax.axis_index("line")
     devices = samp * line
+    pixels = lines * width
+    first, last = me == 0, me == samp - 1
     flat = me * line + ln
     packs = pixels // LANES
     padded = xs.shape[0]
@@ -30,6 +89,45 @@
         other = lax.rem(flat + d, devices)
         return {"samp": other // line, "line": lax.rem(other, line)}
 
+    def line_copy(level, src, dst, tall, wide):
+        rows = RIM * wide
+        start = pl.multiple_of((1 - ln) * ((tall - RIM) * wide), 8)
+        copy = pltpu.make_async_remote_copy(src.at[:, pl.ds(start, rows)], dst, l_send.at[level], l_recv.at[level],
+                                            device_id={"line": 1 - ln}, device_id_type=MESH)
+        copy.start()
+        return copy
+
+    def rim_copies(level, left, right, from_left, from_right):
+        below = pltpu.make_async_remote_copy(left, from_right, r_send.at[level, 0], r_recv.at[level, 0],
+                                             device_id={"samp": jnp.maximum(me - 1, 0)}, device_id_type=MESH)
+        above = pltpu.make_async_remote_copy(right, from_left, r_send.at[level, 1], r_recv.at[level, 1],
+                                             device_id={"samp": jnp.minimum(me + 1, samp - 1)}, device_id_type=MESH)
+
+        @pl.when(me > 0)
+        def _():
+            below.start()
+
+        @pl.when(me < samp - 1)
+        def _():
+            above.start()
+
+        return below, above
+
+    def rim_wait(pair):
+        below, above = pair
+
+        @pl.when(me > 0)
+        def _():
+            below.wait_send()
+            above.wait_recv()
+
+        @pl.when(me < samp - 1)
+        def _():
+            above.wait_send()
+            below.wait_recv()
+
+    for ref in (fl1, fr1, fl2, fr2, fl3, fr3):
+        ref[...] = jnp.zeros_like(ref)
     barrier = pltpu.get_barrier_semaphore()
     for d in range(1, devices):
         pl.semaphore_signal(barrier, inc=1, device_id=peer(d), device_id_type=MESH)
@@ -53,7 +151,9 @@
         total = total + sums_in[d - 1]
     mean = jnp.transpose(total / float(pixels * devices))[:, 0:1]
     xs[...] = xs[...] - mean
-    xc_ref[...] = xs[0:bands, :]
+    for t in range(v1.shape[0]):
+        v1[t] = jnp.transpose(xs[t * LANES:(t + 1) * LANES, :])
+    lines1 = line_copy(0, v1, n1, lines, width)
     rows, offsets = blocks_of(bands)
     for q, (count, offset) in enumerate(zip(rows, offsets)):
         g[offset:offset + count, :] = lax.dot_general(
@@ -72,6 +172,9 @@
             h_recv.at[d - 1], device_id={"line": other}, device_id_type=MESH)
         copy.start()
         copies.append(copy)
+    lines1.wait()
+    lift_lines(v1, n1, z1, lines, width, ln)
+    rims(z1, lines, width, el1, er1)
     for copy in copies:
         copy.wait()
     mine = pl.ds(pl.multiple_of(ln * half, 8), half)
@@ -87,6 +190,16 @@
             c_send.at[d - 1], c_recv.at[d - 1], device_id={"samp": other}, device_id_type=MESH)
         copy.start()
         copies.append(copy)
+    pair = rim_copies(0, el1, er1, fl1, fr1)
+    rim_wait(pair)
+    h, w = lines // 2, width // 2
+    one = h * w
+    lift_samples(z1, fl1, fr1, lines, width, first, last, ((v2, 0), (t_ref, 0), (t_ref, one), (t_ref, 2 * one)))
+    lines2 = line_copy(1, v2, n2, h, w)
+    lines2.wait()
+    lift_lines(v2, n2, z2, h, w, ln)
+    rims(z2, h, w, el2, er2)
+    pair2 = rim_copies(1, el2, er2, fl2, fr2)
     for copy in copies:
         copy.wait()
     own = pl.ds(pl.multiple_of(ln * half + me * chunk, 8), chunk)
@@ -101,6 +214,16 @@
                                             device_id={"samp": other}, device_id_type=MESH)
         copy.start()
         copies.append(copy)
+    rim_wait(pair2)
+    two, base2 = one // 4, 3 * one
+    lift_samples(z2, fl2, fr2, h, w, first, last,
+                 ((v3, 0), (t_ref, base2), (t_ref, base2 + two), (t_ref, base2 + 2 * two)))
+    h, w = h // 2, w // 2
+    lines3 = line_copy(2, v3, n3, h, w)
+    lines3.wait()
+    lift_lines(v3, n3, z3, h, w, ln)
+    rims(z3, h, w, el3, er3)
+    pair3 = rim_copies(2, el3, er3, fl3, fr3)
     for copy in copies:
         copy.wait()
     copies = []
@@ -110,12 +233,17 @@
                                             device_id={"line": other}, device_id_type=MESH)
         copy.start()
         copies.append(copy)
+    rim_wait(pair3)
+    three, base3 = two // 4, base2 + 3 * two
+    lift_samples(z3, fl3, fr3, h, w, first, last,
+                 ((t_ref, base3 + 3 * three), (t_ref, base3), (t_ref, base3 + three), (t_ref, base3 + 2 * three)))
     for copy in copies:
         copy.wait()
     p_ref[...] = tot[...]
 
 
-def gram_call(cube, bands, pixels):
+def gram_call(cube, bands, lines, width):
+    pixels = lines * width
     samp, line = lax.axis_size("samp"), lax.axis_size("line")
     devices = samp * line
     rows, offsets = blocks_of(bands)
@@ -126,11 +254,17 @@
     f32 = jnp.float32
     sem = pltpu.SemaphoreType.DMA
     return pl.pallas_call(
-        functools.partial(gram_kernel, samp, line, bands, pixels),
-        out_shape=(jax.ShapeDtypeStruct((bands, pixels), f32), jax.ShapeDtypeStruct((total, LANES), f32)),
+        functools.partial(gram_kernel, samp, line, bands, lines, width),
+        out_shape=(jax.ShapeDtypeStruct((padded // LANES, pixels, LANES), f32), jax.ShapeDtypeStruct((total, LANES), f32)),
         in_specs=[pl.BlockSpec(memory_space=pltpu.VMEM)],
         out_specs=(pl.BlockSpec(memory_space=pltpu.VMEM), pl.BlockSpec(memory_space=pltpu.VMEM)),
         scratch_shapes=[
+            *[pltpu.VMEM((padded // LANES, pixels // 4 ** i, LANES), f32) for i in (0, 1, 2)],
+            *[pltpu.VMEM((padded // LANES, pixels // 4 ** i, LANES), f32) for i in (0, 1, 2)],
+            *[pltpu.VMEM((padded // LANES, RIM * width // 2 ** i, LANES), f32) for i in (0, 1, 2)],
+            *[pltpu.VMEM((padded // LANES, RIM * lines // 2 ** i, LANES), f32) for i in (0, 0, 1, 1, 2, 2)],
+            *[pltpu.VMEM((padded // LANES, RIM * lines // 2 ** i, LANES), f32) for i in (0, 0, 1, 1, 2, 2)],
+            sem((3,)), sem((3,)), sem((3, 2)), sem((3, 2)),
             pltpu.VMEM((padded, pixels), f32), pltpu.VMEM((8, padded), f32),
             pltpu.VMEM((devices - 1, 8, padded), f32), pltpu.VMEM((total, LANES), f32),
             pltpu.VMEM((line - 1, total // line, LANES), f32),
@@ -150,7 +284,7 @@
     return first, second, rest - second
 
 
-def inverse_kernel(bands, count, p_ref, w_ref, m):
+def inverse_kernel(bands, count, p_ref, t_ref, o1_ref, rest_ref, m):
     wide = m.shape[1]
     rows, offsets = blocks_of(bands)
     diag = lax.broadcasted_iota(jnp.int32, (LANES, LANES), 0) == lax.broadcasted_iota(
@@ -249,132 +383,42 @@
         lax.fori_loop(0, min(LANES, span) // 8, step, 0)
     keep = lax.broadcasted_iota(jnp.int32, (bands, wide), 1) <= lax.broadcasted_iota(
         jnp.int32, (bands, wide), 0)
-    w_ref[...] = jnp.where(keep, m[...], 0.0)[:, :bands]
-
-
-def inverse_call(packed, bands, count):
+    m[...] = jnp.where(keep, m[...], 0.0)
+    for q in range(t_ref.shape[1] // LANES):
+        part = jnp.concatenate([t_ref[t, q * LANES:(q + 1) * LANES, :] for t in range(wide // LANES)], axis=1)
+        out = lax.dot_general(m[...], part, (((1,), (1,)), ((), ())),
+                              precision=HIGH, preferred_element_type=jnp.float32)
+        if q < o1_ref.shape[0]:
+            o1_ref[q] = out
+        else:
+            rest_ref[...] = out
+
+
+def inverse_call(packed, coefs, bands, count):
     wide = -(-bands // LANES) * LANES
+    f32 = jnp.float32
+    vmem = pl.BlockSpec(memory_space=pltpu.VMEM)
     return pl.pallas_call(
         functools.partial(inverse_kernel, bands, count),
-        out_shape=jax.ShapeDtypeStruct((bands, bands), jnp.float32),
-        in_specs=[pl.BlockSpec(memory_space=pltpu.VMEM)],
-        out_specs=pl.BlockSpec(memory_space=pltpu.VMEM),
-        scratch_shapes=[pltpu.VMEM((bands, wide), jnp.float32)],
-    )(packed)
-
-BANDS = 432
-LD = 32
-SD = 16
-
-
-alpha_lift = -1.586134342059924
-beta_lift = -0.052980118572961
-gamma_lift = 0.882911075530934
-delta_lift = 0.443506852043971
-scale_lift = 1.230174104914001
-
-
-def passed_along(array, axis, by):
-    count = lax.axis_size(axis)
-    pairs = [(i, i + by) for i in range(count) if 0 <= i + by < count]
-    return lax.ppermute(array, axis, pairs)
-
-
-def with_halo(block, sides, width):
-    for axis, dim in sides:
-        count = lax.axis_size(axis)
-        forward = [(i, i + 1) for i in range(count - 1)]
-        backward = [(target, source) for source, target in forward]
-        low = lax.ppermute(
-            lax.slice_in_dim(block, block.shape[dim] - width, None, axis=dim), axis, forward
-        )
-        high = lax.ppermute(lax.slice_in_dim(block, 0, width, axis=dim), axis, backward)
-        block = jnp.concatenate([low, block, high], axis=dim)
-    return block
-
-
-def lines_next(edge):
-    return passed_along(edge, "line", -1)
-
-
-def lines_prev(edge):
-    return passed_along(edge, "line", 1)
-
-
-def split_pairs(values, axis):
-    length = values.shape[axis]
-    return (
-        lax.slice_in_dim(values, 0, length, 2, axis),
-        lax.slice_in_dim(values, 1, length, 2, axis),
-    )
-
-
-def lift_steps(values, axis, fetch_next, fetch_prev, at_first, at_last):
-    evens, odds = split_pairs(values, axis)
-    half = evens.shape[axis]
-    for weight_odd, weight_even in ((alpha_lift, beta_lift), (gamma_lift, delta_lift)):
-        own_last = lax.slice_in_dim(evens, half - 1, half, 1, axis)
-        arrived = fetch_next(lax.slice_in_dim(evens, 0, 1, 1, axis))
-        beyond = jnp.where(at_last, own_last, arrived)
-        following = jnp.concatenate([lax.slice_in_dim(evens, 1, half, 1, axis), beyond], axis)
-        odds = odds + weight_odd * (evens + following)
-        own_first = lax.slice_in_dim(odds, 0, 1, 1, axis)
-        received = fetch_prev(lax.slice_in_dim(odds, half - 1, half, 1, axis))
-        before = jnp.where(at_first, own_first, received)
-        preceding = jnp.concatenate([before, lax.slice_in_dim(odds, 0, half - 1, 1, axis)], axis)
-        evens = evens + weight_even * (preceding + odds)
-    return (evens / scale_lift, odds * scale_lift)
-
-
-def lift_rims(values, at_first, at_last):
-    length = values.shape[2]
-    widened = with_halo(values, (("samp", 2),), 4)
-    from_left = widened[:, :, :4]
-    from_right = widened[:, :, length + 4 :]
-    with_right = jnp.concatenate([values, from_right], 2)
-    with_left = jnp.concatenate([from_left, values], 2)
-    left_mirror = jnp.flip(with_right[:, :, 1:5], axis=2)
-    right_mirror = jnp.flip(with_left[:, :, length - 1 : length + 3], axis=2)
-    left_rim = jnp.where(at_first, left_mirror, from_left)
-    right_rim = jnp.where(at_last, right_mirror, from_right)
-    extended = jnp.concatenate([left_rim, values, right_rim], 2)
-    evens, odds = split_pairs(extended, 2)
-    odds = odds[..., :-1] + alpha_lift * (evens[..., :-1] + evens[..., 1:])
-    evens = evens[..., 1:-1] + beta_lift * (odds[..., :-1] + odds[..., 1:])
-    odds = odds[..., 1:-1] + gamma_lift * (evens[..., :-1] + evens[..., 1:])
-    evens = evens[..., 1:-1] + delta_lift * (odds[..., :-1] + odds[..., 1:])
-    return (evens / scale_lift, odds[..., 1:] * scale_lift)
+        out_shape=(jax.ShapeDtypeStruct((3, bands, LANES), f32), jax.ShapeDtypeStruct((bands, LANES), f32)),
+        in_specs=[vmem, vmem],
+        out_specs=(vmem, vmem),
+        scratch_shapes=[pltpu.VMEM((bands, wide), f32)],
+    )(packed, coefs)
 
 
 def local(cube):
-    band_count = BANDS
-    line_count = LD
-    samples = SD
-    tile = cube.reshape(band_count, line_count, samples)
-    pixels = line_count * samples
+    pixels = LD * SD
     devices = lax.axis_size("samp") * lax.axis_size("line")
-    centered, packed = gram_call(cube, band_count, pixels)
-    whitener = inverse_call(packed, band_count, pixels * devices)
-    components = jnp.dot(
-        whitener, centered, precision=lax.Precision.HIGHEST, preferred_element_type=jnp.float32
-    ).reshape(tile.shape)
-    samp_first = lax.axis_index("samp") == 0
-    samp_last = lax.axis_index("samp") == lax.axis_size("samp") - 1
-    line_first = lax.axis_index("line") == 0
-    line_last = lax.axis_index("line") == lax.axis_size("line") - 1
-
-    def decompose(values):
-        low_s, high_s = lift_rims(values, samp_first, samp_last)
-        joined = jnp.concatenate([low_s, high_s], 2)
-        low_l, high_l = lift_steps(joined, 1, lines_next, lines_prev, line_first, line_last)
-        middle = low_s.shape[2]
-        details = jnp.stack([high_l[:, :, :middle], low_l[:, :, middle:], high_l[:, :, middle:]])
-        return (low_l[:, :, :middle], details)
-
-    approx1, details1 = decompose(components)
-    approx2, details2 = decompose(approx1)
-    approx3, details3 = decompose(approx2)
-    return (details1.reshape(-1), details2.reshape(-1), details3.reshape(-1), approx3.reshape(-1))
+    coefs, packed = gram_call(cube, BANDS, LD, SD)
+    first, rest = inverse_call(packed, coefs, BANDS, pixels * devices)
+    second = pixels // 16
+    third = second // 4
+    level2 = [rest[:, i * second:(i + 1) * second] for i in range(3)]
+    base = 3 * second
+    level3 = [rest[:, base + i * third:base + (i + 1) * third] for i in range(3)]
+    approx = rest[:, base + 3 * third:base + 4 * third]
+    return (first.reshape(-1), jnp.stack(level2).reshape(-1), jnp.stack(level3).reshape(-1), approx.reshape(-1))
 
 
 def solution(mesh):

time: 185 us -> 91.1 us (0.49); the launches traced: 183 us -> 90.9 us
  starting transfers between devices: 39.4 us -> 0 us
  local copies, waits for them, and re-layouts: 37.4 us -> 4.21 us
  waiting for transfers between devices: 29.8 us -> 0 us
  Pallas kernels: 66.7 us -> 85.9 us
  other arithmetic: 4.89 us -> 0.09 us
  matrix products: 3.08 us -> 0 us
    ppermute x18 -> x0, starting transfers between devices: 39.4 us -> none  [the longest x12 22.1 us: passed_along(): return lax.ppermute(array, axis, pairs)]
    ppermute x18 -> x0, waiting for transfers between devices: 29.8 us -> none  [the longest x3 12.2 us: with_halo(): lax.ppermute(lax.slice_in_dim(block, block.shape[dim] - width, None, axis...]
    reshape x4 -> x3, local copies, waits for them, and re-layouts: 19.5 us -> 2.54 us  [the longest x1 0.92 us: local(): jnp.stack(level3).reshape(-1)]
    pallas_call x1, Pallas kernels: 34.2 us -> 50.3 us  [gram_call(): pl.pallas_call(functools.partial(gram_kernel, samp, line, bands, lines, w...]
    another operation x6 -> x1, local copies, waits for them, and re-layouts: 11 us -> 1.33 us  [local(): jnp.stack(level2).reshape(-1)]
    slice x39 -> x1, local copies, waits for them, and re-layouts: 5.15 us -> 0.29 us  [local(): approx = rest[:, base + 3 * third:base + 4 * third]]
    pallas_call x1, Pallas kernels: 32.5 us -> 35.6 us  [inverse_call(): pl.pallas_call(functools.partial(inverse_kernel, bands, count), out_shape...]
    dot_general x1 -> x0, matrix products: 3.08 us -> none  [local(): jnp.dot(whitener, centered, precision=lax.Precision.HIGHEST, preferred_el...]
  transfers between devices with their start and end apart: 18 -> 0, of which waited for: 15 -> 0; matrix products, arithmetic and copies ran while one was open for 15% -> 0% of each run, Pallas kernels for 0% -> 0%
where the time goes in v1:
time: 91.1 us; the launch traced here: 90.9 us
  Pallas kernels  85.9 us (94%)
  local copies, waits for them, and re-layouts  4.21 us (5%)
    pallas_call x1, Pallas kernels, gram_call(): pl.pallas_call(functools.partial(gram_kernel, samp, line, bands, lines, w...  50.3 us
    pallas_call x1, Pallas kernels, inverse_call(): pl.pallas_call(functools.partial(inverse_kernel, bands, count), out_shape...  35.6 us

profile of v1, /device:TPU:0, one launch (start us, length us, event | category | flops | bytes accessed | tf_op | source)
XLA Modules:
  0.0 90.9 jit_solution(9969234068920606346)
XLA Ops:
  0.6 50.3 %shard_map.46 = (f32[4,512,128]{2,1,0:T(8,128)}, f32[1024,128]{1,0:T(8,128)}) custom-call(f32[1728,128]{1,0:T(8,128)} %bitcast.14), custom_call_target="tpu_custom_call" | custom-call | tf_op jit(solution)/shard_map/pallas_call | solution.py:256
  51.0 35.6 %shard_map.47 = (f32[3,432,128]{2,1,0:T(8,128)}, f32[432,128]{1,0:T(8,128)}) custom-call(f32[1024,128]{1,0:T(8,128)} %get-tuple-element.8.p_ref, f32[4,512,128]{2,1,0:T(8,128)} %get-tuple-element.9.t_ref), custom_call_target="tpu_custom_call" | custom-call | tf_op jit(solution)/shard_map/pallas_call | solution.py:401
  86.6 1.3 %slice_bitcast_fusion.5 = (f32[1,432,32]{2,1,0:T(8,128)S(1)}, f32[1,432,32]{2,1,0:T(8,128)S(1)}, f32[1,432,32]{2,1,0:T(8,128)S(1)}) fusion(f32[432,128]{1,0:T(8,128)} %get-tuple-element.11), kind=kLoop, calls=%fused_computation.7 | loop fusion | bytes 331776 | tf_op jit(solution)/shard_map/stack | solution.py:421
  87.9 0.0 copy-start
  88.0 0.9 reshape.25
  88.8 0.1 copy-done
  88.9 0.3 fusion
  89.2 0.8 reshape.27
  90.0 0.9 %reshape.26 = f32[10368]{0:T(1024)} reshape(f32[3,432,8]{2,1,0:T(8,128)S(1)} %pad_maximum_fusion.1) | data formatting | bytes 82944 | tf_op jit(solution)/shard_map/reshape | solution.py:421
  (2 shorter events, 0.1 us)
Async XLA Ops:
  87.9 0.9 %copy-start = (f32[432,128]{1,0:T(8,128)S(1)}, f32[432,128]{1,0:T(8,128)}, u32[]{:S(2)}) copy-start(f32[432,128]{1,0:T(8,128)} %get-tuple-element.11) | copy-start | bytes 663556

commit v2 on v1

--- a/solution.py
+++ b/solution.py
@@ -73,7 +73,14 @@
                 ref[t, pl.ds(base + i, half, stride=width // 2), :] = value
 
 
-def gram_kernel(samp, line, bands, lines, width, x_ref, t_ref, p_ref, v1, v2, v3, z1, z2, z3, n1, n2, n3, el1, er1, el2, er2, el3, er3, fl1, fr1, fl2, fr2, fl3, fr3,
+def split3(value):
+    first = value.astype(jnp.bfloat16).astype(jnp.float32)
+    rest = value - first
+    second = rest.astype(jnp.bfloat16).astype(jnp.float32)
+    return first, second, rest - second
+
+
+def gram_kernel(samp, line, bands, lines, width, x_ref, o1_ref, o2_ref, o3_ref, o4_ref, t_ref, m, rest, v1, v2, v3, z1, z2, z3, n1, n2, n3, el1, er1, el2, er2, el3, er3, fl1, fr1, fl2, fr2, fl3, fr3,
                 l_send, l_recv, r_send, r_recv, xs, sums, sums_in, g, half_in,
                 chunk_in, tot, s_send, s_recv, h_send, h_recv, c_send, c_recv, a_send, a_recv,
                 b_send, b_recv):
@@ -136,7 +143,7 @@
     for q in range(packs):
         xs[0:bands, q * LANES:(q + 1) * LANES] = x_ref[pl.ds(q, bands, stride=packs), :]
     sums[...] = lax.dot_general(jnp.ones((8, pixels), jnp.float32), xs[...], (((1,), (1,)), ((), ())),
-                                precision=HIGH, preferred_element_type=jnp.float32)
+                                precision=HIGH, preferred_element_type=jnp.float32)[0:1]
     pl.semaphore_wait(barrier, devices - 1)
     copies = []
     for d in range(1, devices):
@@ -149,11 +156,8 @@
     total = sums[...]
     for d in range(1, devices):
         total = total + sums_in[d - 1]
-    mean = jnp.transpose(total / float(pixels * devices))[:, 0:1]
+    mean = jnp.transpose(jnp.broadcast_to(total / float(pixels * devices), (8, padded)))[:, 0:1]
     xs[...] = xs[...] - mean
-    for t in range(v1.shape[0]):
-        v1[t] = jnp.transpose(xs[t * LANES:(t + 1) * LANES, :])
-    lines1 = line_copy(0, v1, n1, lines, width)
     rows, offsets = blocks_of(bands)
     for q, (count, offset) in enumerate(zip(rows, offsets)):
         g[offset:offset + count, :] = lax.dot_general(
@@ -172,9 +176,9 @@
             h_recv.at[d - 1], device_id={"line": other}, device_id_type=MESH)
         copy.start()
         copies.append(copy)
-    lines1.wait()
-    lift_lines(v1, n1, z1, lines, width, ln)
-    rims(z1, lines, width, el1, er1)
+    for t in range(v1.shape[0]):
+        v1[t] = jnp.transpose(xs[t * LANES:(t + 1) * LANES, :])
+    lines1 = line_copy(0, v1, n1, lines, width)
     for copy in copies:
         copy.wait()
     mine = pl.ds(pl.multiple_of(ln * half, 8), half)
@@ -190,16 +194,9 @@
             c_send.at[d - 1], c_recv.at[d - 1], device_id={"samp": other}, device_id_type=MESH)
         copy.start()
         copies.append(copy)
-    pair = rim_copies(0, el1, er1, fl1, fr1)
-    rim_wait(pair)
-    h, w = lines // 2, width // 2
-    one = h * w
-    lift_samples(z1, fl1, fr1, lines, width, first, last, ((v2, 0), (t_ref, 0), (t_ref, one), (t_ref, 2 * one)))
-    lines2 = line_copy(1, v2, n2, h, w)
-    lines2.wait()
-    lift_lines(v2, n2, z2, h, w, ln)
-    rims(z2, h, w, el2, er2)
-    pair2 = rim_copies(1, el2, er2, fl2, fr2)
+    lines1.wait()
+    lift_lines(v1, n1, z1, lines, width, ln)
+    rims(z1, lines, width, el1, er1)
     for copy in copies:
         copy.wait()
     own = pl.ds(pl.multiple_of(ln * half + me * chunk, 8), chunk)
@@ -214,16 +211,7 @@
                                             device_id={"samp": other}, device_id_type=MESH)
         copy.start()
         copies.append(copy)
-    rim_wait(pair2)
-    two, base2 = one // 4, 3 * one
-    lift_samples(z2, fl2, fr2, h, w, first, last,
-                 ((v3, 0), (t_ref, base2), (t_ref, base2 + two), (t_ref, base2 + 2 * two)))
-    h, w = h // 2, w // 2
-    lines3 = line_copy(2, v3, n3, h, w)
-    lines3.wait()
-    lift_lines(v3, n3, z3, h, w, ln)
-    rims(z3, h, w, el3, er3)
-    pair3 = rim_copies(2, el3, er3, fl3, fr3)
+    pair = rim_copies(0, el1, er1, fl1, fr1)
     for copy in copies:
         copy.wait()
     copies = []
@@ -233,67 +221,17 @@
                                             device_id={"line": other}, device_id_type=MESH)
         copy.start()
         copies.append(copy)
-    rim_wait(pair3)
-    three, base3 = two // 4, base2 + 3 * two
-    lift_samples(z3, fl3, fr3, h, w, first, last,
-                 ((t_ref, base3 + 3 * three), (t_ref, base3), (t_ref, base3 + three), (t_ref, base3 + 2 * three)))
     for copy in copies:
         copy.wait()
-    p_ref[...] = tot[...]
-
-
-def gram_call(cube, bands, lines, width):
-    pixels = lines * width
-    samp, line = lax.axis_size("samp"), lax.axis_size("line")
-    devices = samp * line
-    rows, offsets = blocks_of(bands)
-    used = offsets[-1] + rows[-1]
-    unit = 8 * devices
-    total = -(-used // unit) * unit
-    padded = -(-bands // LANES) * LANES
-    f32 = jnp.float32
-    sem = pltpu.SemaphoreType.DMA
-    return pl.pallas_call(
-        functools.partial(gram_kernel, samp, line, bands, lines, width),
-        out_shape=(jax.ShapeDtypeStruct((padded // LANES, pixels, LANES), f32), jax.ShapeDtypeStruct((total, LANES), f32)),
-        in_specs=[pl.BlockSpec(memory_space=pltpu.VMEM)],
-        out_specs=(pl.BlockSpec(memory_space=pltpu.VMEM), pl.BlockSpec(memory_space=pltpu.VMEM)),
-        scratch_shapes=[
-            *[pltpu.VMEM((padded // LANES, pixels // 4 ** i, LANES), f32) for i in (0, 1, 2)],
-            *[pltpu.VMEM((padded // LANES, pixels // 4 ** i, LANES), f32) for i in (0, 1, 2)],
-            *[pltpu.VMEM((padded // LANES, RIM * width // 2 ** i, LANES), f32) for i in (0, 1, 2)],
-            *[pltpu.VMEM((padded // LANES, RIM * lines // 2 ** i, LANES), f32) for i in (0, 0, 1, 1, 2, 2)],
-            *[pltpu.VMEM((padded // LANES, RIM * lines // 2 ** i, LANES), f32) for i in (0, 0, 1, 1, 2, 2)],
-            sem((3,)), sem((3,)), sem((3, 2)), sem((3, 2)),
-            pltpu.VMEM((padded, pixels), f32), pltpu.VMEM((8, padded), f32),
-            pltpu.VMEM((devices - 1, 8, padded), f32), pltpu.VMEM((total, LANES), f32),
-            pltpu.VMEM((line - 1, total // line, LANES), f32),
-            pltpu.VMEM((samp - 1, total // devices, LANES), f32), pltpu.VMEM((total, LANES), f32),
-            sem((devices - 1,)), sem((devices - 1,)), sem((line - 1,)), sem((line - 1,)),
-            sem((samp - 1,)), sem((samp - 1,)), sem((samp - 1,)), sem((samp - 1,)),
-            sem((line - 1,)), sem((line - 1,)),
-        ],
-        compiler_params=pltpu.CompilerParams(collective_id=0, has_side_effects=True),
-    )(cube.reshape(-1, LANES))
-
-
-def split3(value):
-    first = value.astype(jnp.bfloat16).astype(jnp.float32)
-    rest = value - first
-    second = rest.astype(jnp.bfloat16).astype(jnp.float32)
-    return first, second, rest - second
-
-
-def inverse_kernel(bands, count, p_ref, t_ref, o1_ref, rest_ref, m):
     wide = m.shape[1]
     rows, offsets = blocks_of(bands)
     diag = lax.broadcasted_iota(jnp.int32, (LANES, LANES), 0) == lax.broadcasted_iota(
         jnp.int32, (LANES, LANES), 1)
-    scale = 1.0 / float(count)
+    scale = 1.0 / float(pixels * devices)
     trace = jnp.zeros((1, 1), jnp.float32)
     for q, offset in enumerate(offsets):
         size = min(LANES, rows[q])
-        block = p_ref[offset:offset + size, :]
+        block = tot[offset:offset + size, :]
         kept = jnp.where(diag[:size], block, 0.0)
         trace = trace + jnp.sum(jnp.sum(kept, axis=0, keepdims=True), axis=1, keepdims=True)
     ridge = trace * scale * (0.01 / bands)
@@ -301,7 +239,7 @@
         for b in range(q, len(rows)):
             size = min(LANES, rows[b])
             start = offset + (b - q) * LANES
-            block = p_ref[start:start + size, :] * scale
+            block = tot[start:start + size, :] * scale
             if b == q:
                 low = jnp.where(diag[:size], block + ridge, block)
                 m[q * LANES:q * LANES + size, q * LANES:(q + 1) * LANES] = low
@@ -313,7 +251,7 @@
     sub = lax.broadcasted_iota(jnp.int32, (8, LANES), 0)
     lane = lax.broadcasted_iota(jnp.int32, (8, LANES), 1)
 
-    for c in range(len(rows)):
+    def eliminate(c):
         top = c * LANES
         span = bands - top
 
@@ -381,6 +319,34 @@
             return carry
 
         lax.fori_loop(0, min(LANES, span) // 8, step, 0)
+    eliminate(0)
+    rim_wait(pair)
+    h, w = lines // 2, width // 2
+    one = h * w
+    lift_samples(z1, fl1, fr1, lines, width, first, last, ((v2, 0), (t_ref, 0), (t_ref, one), (t_ref, 2 * one)))
+    lines2 = line_copy(1, v2, n2, h, w)
+    eliminate(1)
+    lines2.wait()
+    lift_lines(v2, n2, z2, h, w, ln)
+    rims(z2, h, w, el2, er2)
+    pair2 = rim_copies(1, el2, er2, fl2, fr2)
+    eliminate(2)
+    rim_wait(pair2)
+    two, base2 = one // 4, 3 * one
+    lift_samples(z2, fl2, fr2, h, w, first, last,
+                 ((v3, 0), (t_ref, base2), (t_ref, base2 + two), (t_ref, base2 + 2 * two)))
+    h, w = h // 2, w // 2
+    lines3 = line_copy(2, v3, n3, h, w)
+    lines3.wait()
+    lift_lines(v3, n3, z3, h, w, ln)
+    rims(z3, h, w, el3, er3)
+    pair3 = rim_copies(2, el3, er3, fl3, fr3)
+    for c in range(3, len(rows)):
+        eliminate(c)
+    rim_wait(pair3)
+    three, base3 = two // 4, base2 + 3 * two
+    lift_samples(z3, fl3, fr3, h, w, first, last,
+                 ((t_ref, base3 + 3 * three), (t_ref, base3), (t_ref, base3 + three), (t_ref, base3 + 2 * three)))
     keep = lax.broadcasted_iota(jnp.int32, (bands, wide), 1) <= lax.broadcasted_iota(
         jnp.int32, (bands, wide), 0)
     m[...] = jnp.where(keep, m[...], 0.0)
@@ -391,34 +357,63 @@
         if q < o1_ref.shape[0]:
             o1_ref[q] = out
         else:
-            rest_ref[...] = out
-
-
-def inverse_call(packed, coefs, bands, count):
-    wide = -(-bands // LANES) * LANES
+            rest[...] = out
+
+
+    def pack(dest, at, lane0, wide_out):
+        group = LANES // wide_out
+        count = bands // group
+        pieces = [rest[pl.ds(b, count, stride=group), :][:, lane0:lane0 + wide_out] for b in range(group)]
+        dest[at:at + count, :] = jnp.concatenate(pieces, axis=1)
+
+    for i in range(3):
+        pack(o2_ref, i * (o2_ref.shape[0] // 3), i * two, two)
+        pack(o3_ref, i * (o3_ref.shape[0] // 3), 3 * two + i * three, three)
+    pack(o4_ref, 0, 3 * two + 3 * three, three)
+
+
+def gram_call(cube, bands, lines, width):
+    pixels = lines * width
+    samp, line = lax.axis_size("samp"), lax.axis_size("line")
+    devices = samp * line
+    rows, offsets = blocks_of(bands)
+    used = offsets[-1] + rows[-1]
+    unit = 8 * devices
+    total = -(-used // unit) * unit
+    padded = -(-bands // LANES) * LANES
     f32 = jnp.float32
-    vmem = pl.BlockSpec(memory_space=pltpu.VMEM)
+    sem = pltpu.SemaphoreType.DMA
     return pl.pallas_call(
-        functools.partial(inverse_kernel, bands, count),
-        out_shape=(jax.ShapeDtypeStruct((3, bands, LANES), f32), jax.ShapeDtypeStruct((bands, LANES), f32)),
-        in_specs=[vmem, vmem],
-        out_specs=(vmem, vmem),
-        scratch_shapes=[pltpu.VMEM((bands, wide), f32)],
-    )(packed, coefs)
+        functools.partial(gram_kernel, samp, line, bands, lines, width),
+        out_shape=(jax.ShapeDtypeStruct((3, bands, LANES), f32),
+                   jax.ShapeDtypeStruct((3 * bands * (pixels // 16) // LANES, LANES), f32),
+                   jax.ShapeDtypeStruct((3 * bands * (pixels // 64) // LANES, LANES), f32),
+                   jax.ShapeDtypeStruct((bands * (pixels // 64) // LANES, LANES), f32)),
+        in_specs=[pl.BlockSpec(memory_space=pltpu.VMEM)],
+        out_specs=(pl.BlockSpec(memory_space=pltpu.VMEM),) * 4,
+        scratch_shapes=[
+            pltpu.VMEM((padded // LANES, pixels, LANES), f32), pltpu.VMEM((bands, padded), f32),
+            pltpu.VMEM((bands, LANES), f32),
+            *[pltpu.VMEM((padded // LANES, pixels // 4 ** i, LANES), f32) for i in (0, 1, 2)],
+            *[pltpu.VMEM((padded // LANES, pixels // 4 ** i, LANES), f32) for i in (0, 1, 2)],
+            *[pltpu.VMEM((padded // LANES, RIM * width // 2 ** i, LANES), f32) for i in (0, 1, 2)],
+            *[pltpu.VMEM((padded // LANES, RIM * lines // 2 ** i, LANES), f32) for i in (0, 0, 1, 1, 2, 2)],
+            *[pltpu.VMEM((padded // LANES, RIM * lines // 2 ** i, LANES), f32) for i in (0, 0, 1, 1, 2, 2)],
+            sem((3,)), sem((3,)), sem((3, 2)), sem((3, 2)),
+            pltpu.VMEM((padded, pixels), f32), pltpu.VMEM((1, padded), f32),
+            pltpu.VMEM((devices - 1, 1, padded), f32), pltpu.VMEM((total, LANES), f32),
+            pltpu.VMEM((line - 1, total // line, LANES), f32),
+            pltpu.VMEM((samp - 1, total // devices, LANES), f32), pltpu.VMEM((total, LANES), f32),
+            sem((devices - 1,)), sem((devices - 1,)), sem((line - 1,)), sem((line - 1,)),
+            sem((samp - 1,)), sem((samp - 1,)), sem((samp - 1,)), sem((samp - 1,)),
+            sem((line - 1,)), sem((line - 1,)),
+        ],
+        compiler_params=pltpu.CompilerParams(collective_id=0, has_side_effects=True),
+    )(cube.reshape(-1, LANES))
 
 
 def local(cube):
-    pixels = LD * SD
-    devices = lax.axis_size("samp") * lax.axis_size("line")
-    coefs, packed = gram_call(cube, BANDS, LD, SD)
-    first, rest = inverse_call(packed, coefs, BANDS, pixels * devices)
-    second = pixels // 16
-    third = second // 4
-    level2 = [rest[:, i * second:(i + 1) * second] for i in range(3)]
-    base = 3 * second
-    level3 = [rest[:, base + i * third:base + (i + 1) * third] for i in range(3)]
-    approx = rest[:, base + 3 * third:base + 4 * third]
-    return (first.reshape(-1), jnp.stack(level2).reshape(-1), jnp.stack(level3).reshape(-1), approx.reshape(-1))
+    return tuple(out.reshape(-1) for out in gram_call(cube, BANDS, LD, SD))
 
 
 def solution(mesh):

time: 91.1 us -> 73.1 us (0.80)
  Pallas kernels: 85.9 us -> 68 us
    pallas_call x1 -> x0, Pallas kernels: 35.6 us -> none  [inverse_call(): pl.pallas_call(functools.partial(inverse_kernel, bands, count), out_shape...]
    pallas_call x1, Pallas kernels: 50.3 us -> 68 us  [gram_call(): pl.pallas_call(functools.partial(gram_kernel, samp, line, bands, lines, w...]
    unnamed x2 -> x10, local copies, waits for them, and re-layouts: 0.06 us -> 4.12 us
    reshape x3 -> x0, local copies, waits for them, and re-layouts: 2.54 us -> none  [the longest x1 0.92 us: local(): jnp.stack(level3).reshape(-1)]
    another operation x1 -> x0, local copies, waits for them, and re-layouts: 1.33 us -> none  [local(): jnp.stack(level2).reshape(-1)]
where the time goes in v2:
time: 73.1 us; the launch traced here: 72.8 us
  Pallas kernels  68 us (93%)
  local copies, waits for them, and re-layouts  4.12 us (6%)
    pallas_call x1, Pallas kernels, gram_call(): pl.pallas_call(functools.partial(gram_kernel, samp, line, bands, lines, w...  68 us
    unnamed x10, local copies, waits for them, and re-layouts  4.12 us

profile of v2, /device:TPU:0, one launch (start us, length us, event | category | flops | bytes accessed | tf_op | source)
XLA Modules:
  0.0 72.8 jit_solution(5207632758079006628)
XLA Ops:
  0.6 68.0 %shard_map.46 = (f32[3,432,128]{2,1,0:T(8,128)}, f32[324,128]{1,0:T(8,128)}, f32[81,128]{1,0:T(8,128)}, f32[27,128]{1,0:T(8,128)}) custom-call(f32[1728,128]{1,0:T(8,128)} %bitcast.5), custom_call_target="tpu_custom_call" | custom-call | tf_op jit(solution)/shard_map/pallas_call | solution.py:386
  68.6 0.0 copy-start
  68.6 2.0 %copy.9 = f32[165888]{0:T(1024)} copy(f32[165888]{0:T(1024)} %bitcast.6) | data formatting | bytes 1327104
  70.6 0.0 copy-done
  70.6 0.0 copy-start.1
  70.7 0.7 copy.10
  71.3 0.1 copy-done.1
  71.4 0.0 copy-start.2
  71.4 0.6 copy.11
  72.1 0.1 copy-done.2
  72.2 0.6 copy.12
Async XLA Ops:
  68.6 2.0 %copy-start = (f32[324,128]{1,0:T(8,128)S(1)}, f32[324,128]{1,0:T(8,128)}, u32[]{:S(2)}) copy-start(f32[324,128]{1,0:T(8,128)} %get-tuple-element.9) | copy-start | bytes 497668
  70.6 0.8 %copy-start.1 = (f32[81,128]{1,0:T(8,128)S(1)}, f32[81,128]{1,0:T(8,128)}, u32[]{:S(2)}) copy-start(f32[81,128]{1,0:T(8,128)} %get-tuple-element.10) | copy-start | bytes 124420
  71.4 0.7 copy-start.2

commit v3 on v2

--- a/solution.py
+++ b/solution.py
@@ -53,24 +53,32 @@
 
 def rims(z, lines, width, left, right):
     for t in range(z.shape[0]):
-        for c in range(RIM):
-            left[t, c * lines:(c + 1) * lines] = z[t, pl.ds(c, lines, stride=width), :]
-            right[t, c * lines:(c + 1) * lines] = z[t, pl.ds(width - RIM + c, lines, stride=width), :]
+        low = [z[t, pl.ds(s, lines, stride=width), :] for s in range(3)]
+        top = [z[t, pl.ds(s, lines, stride=width), :] for s in range(width - 4, width)]
+        left[t, :lines] = low[0]
+        left[t, lines:] = low[0] + beta_lift * (low[1] + alpha_lift * (low[0] + low[2]))
+        right[t, :lines] = top[3] + alpha_lift * top[2]
+        right[t, lines:] = top[2] + beta_lift * (top[1] + alpha_lift * (top[0] + top[2]))
 
 
 def lift_samples(z, from_left, from_right, lines, width, first, last, dests):
-    half = lines // 2
+    half, n = lines // 2, width // 2
     for t in range(z.shape[0]):
-        own = [z[t, pl.ds(s, lines, stride=width), :] for s in range(width)]
-        left = [from_left[t, c * lines:(c + 1) * lines] for c in range(RIM)]
-        right = [from_right[t, c * lines:(c + 1) * lines] for c in range(RIM)]
-        whole = left + own + right
-        before = [jnp.where(first, whole[2 * RIM - i], left[i]) for i in range(RIM)]
-        after = [jnp.where(last, whole[RIM + width - 2 - i], right[i]) for i in range(RIM)]
-        low, high = lift_list(before + own + after)
-        for i in range(width // 2):
-            for (ref, base), value in zip(dests, (low[i][:half], low[i][half:], high[i][:half], high[i][half:])):
-                ref[t, pl.ds(base + i, half, stride=width // 2), :] = value
+        evens = [z[t, pl.ds(2 * i, lines, stride=width), :] for i in range(n)]
+        odds = [z[t, pl.ds(2 * i + 1, lines, stride=width), :] for i in range(n)]
+        beyond = jnp.where(last, evens[-1], from_right[t, :lines])
+        odds1 = [o + alpha_lift * (e + f) for o, e, f in zip(odds, evens, evens[1:] + [beyond])]
+        before = jnp.where(first, odds1[0], from_left[t, :lines] + alpha_lift * evens[0])
+        evens1 = [e + beta_lift * (p + o) for e, p, o in zip(evens, [before] + odds1[:-1], odds1)]
+        beyond = jnp.where(last, evens1[-1], from_right[t, lines:] + beta_lift * odds1[-1])
+        odds2 = [o + gamma_lift * (e + f) for o, e, f in zip(odds1, evens1, evens1[1:] + [beyond])]
+        outside = from_left[t, lines:] + beta_lift * before
+        before = jnp.where(first, odds2[0], before + gamma_lift * (outside + evens1[0]))
+        evens2 = [e + delta_lift * (p + o) for e, p, o in zip(evens1, [before] + odds2[:-1], odds2)]
+        for i in range(n):
+            low, high = evens2[i] * (1.0 / scale_lift), odds2[i] * scale_lift
+            for (ref, base), value in zip(dests, (low[:half], low[half:], high[:half], high[half:])):
+                ref[t, pl.ds(base + i, half, stride=n), :] = value
 
 
 def split3(value):
@@ -80,7 +88,7 @@
     return first, second, rest - second
 
 
-def gram_kernel(samp, line, bands, lines, width, x_ref, o1_ref, o2_ref, o3_ref, o4_ref, t_ref, m, rest, v1, v2, v3, z1, z2, z3, n1, n2, n3, el1, er1, el2, er2, el3, er3, fl1, fr1, fl2, fr2, fl3, fr3,
+def gram_kernel(samp, line, bands, lines, width, x_ref, o1_ref, o2_ref, o3_ref, o4_ref, t_ref, m, rest, corr, v1, v2, v3, z1, z2, z3, n1, n2, n3, el1, er1, el2, er2, el3, er3, fl1, fr1, fl2, fr2, fl3, fr3,
                 l_send, l_recv, r_send, r_recv, xs, sums, sums_in, g, half_in,
                 chunk_in, tot, s_send, s_recv, h_send, h_recv, c_send, c_recv, a_send, a_recv,
                 b_send, b_recv):
@@ -151,13 +159,9 @@
                                             device_id=peer(d), device_id_type=MESH)
         copy.start()
         copies.append(copy)
-    for copy in copies:
-        copy.wait()
-    total = sums[...]
-    for d in range(1, devices):
-        total = total + sums_in[d - 1]
-    mean = jnp.transpose(jnp.broadcast_to(total / float(pixels * devices), (8, padded)))[:, 0:1]
-    xs[...] = xs[...] - mean
+    sum_copies = copies
+    local_mean = sums[...] / float(pixels)
+    xs[...] = xs[...] - jnp.transpose(jnp.broadcast_to(local_mean, (8, padded)))[:, 0:1]
     rows, offsets = blocks_of(bands)
     for q, (count, offset) in enumerate(zip(rows, offsets)):
         g[offset:offset + count, :] = lax.dot_general(
@@ -176,9 +180,6 @@
             h_recv.at[d - 1], device_id={"line": other}, device_id_type=MESH)
         copy.start()
         copies.append(copy)
-    for t in range(v1.shape[0]):
-        v1[t] = jnp.transpose(xs[t * LANES:(t + 1) * LANES, :])
-    lines1 = line_copy(0, v1, n1, lines, width)
     for copy in copies:
         copy.wait()
     mine = pl.ds(pl.multiple_of(ln * half, 8), half)
@@ -194,13 +195,31 @@
             c_send.at[d - 1], c_recv.at[d - 1], device_id={"samp": other}, device_id_type=MESH)
         copy.start()
         copies.append(copy)
+    for copy in sum_copies:
+        copy.wait()
+    total = sums[...]
+    for d in range(1, devices):
+        total = total + sums_in[d - 1]
+    mean = total / float(pixels * devices)
+    spread = jnp.concatenate([local_mean - mean] + [sums_in[d - 1] / float(pixels) - mean
+                                                    for d in range(1, devices)], axis=0)
+    shift = local_mean - mean
+    for t in range(v1.shape[0]):
+        v1[t] = jnp.transpose(xs[t * LANES:(t + 1) * LANES, :]) + shift[:, t * LANES:(t + 1) * LANES]
+    lines1 = line_copy(0, v1, n1, lines, width)
+    for q, (count, offset) in enumerate(zip(rows, offsets)):
+        corr[offset:offset + count, :] = float(pixels) * lax.dot_general(
+            spread, spread[:, q * LANES:(q + 1) * LANES], (((0,), (0,)), ((), ())), precision=HIGH,
+            preferred_element_type=jnp.float32)[q * LANES:q * LANES + count]
+    if g.shape[0] > used:
+        corr[used:, :] = jnp.zeros((g.shape[0] - used, LANES), jnp.float32)
     lines1.wait()
     lift_lines(v1, n1, z1, lines, width, ln)
     rims(z1, lines, width, el1, er1)
     for copy in copies:
         copy.wait()
     own = pl.ds(pl.multiple_of(ln * half + me * chunk, 8), chunk)
-    value = g[own, :]
+    value = g[own, :] + corr[own, :]
     for d in range(1, samp):
         value = value + chunk_in[d - 1]
     tot[own, :] = value
@@ -305,8 +324,8 @@
             l1, l2, l3 = one * keep, two * keep, three * keep
             left = jnp.concatenate([l1, l1, l1, l2, l2, l3], axis=0)[:, top:]
             update = lax.dot_general(
-                jnp.transpose(left).astype(jnp.bfloat16), right.astype(jnp.bfloat16),
-                (((1,), (0,)), ((), ())), preferred_element_type=jnp.float32)
+                left.astype(jnp.bfloat16), right.astype(jnp.bfloat16),
+                (((0,), (0,)), ((), ())), preferred_element_type=jnp.float32)
             for t in range(wide // LANES):
                 part = slice(t * LANES, (t + 1) * LANES)
                 old = m[top:bands, part]
@@ -393,12 +412,12 @@
         out_specs=(pl.BlockSpec(memory_space=pltpu.VMEM),) * 4,
         scratch_shapes=[
             pltpu.VMEM((padded // LANES, pixels, LANES), f32), pltpu.VMEM((bands, padded), f32),
-            pltpu.VMEM((bands, LANES), f32),
+            pltpu.VMEM((bands, LANES), f32), pltpu.VMEM((total, LANES), f32),
             *[pltpu.VMEM((padded // LANES, pixels // 4 ** i, LANES), f32) for i in (0, 1, 2)],
             *[pltpu.VMEM((padded // LANES, pixels // 4 ** i, LANES), f32) for i in (0, 1, 2)],
             *[pltpu.VMEM((padded // LANES, RIM * width // 2 ** i, LANES), f32) for i in (0, 1, 2)],
-            *[pltpu.VMEM((padded // LANES, RIM * lines // 2 ** i, LANES), f32) for i in (0, 0, 1, 1, 2, 2)],
-            *[pltpu.VMEM((padded // LANES, RIM * lines // 2 ** i, LANES), f32) for i in (0, 0, 1, 1, 2, 2)],
+            *[pltpu.VMEM((padded // LANES, 2 * lines // 2 ** i, LANES), f32) for i in (0, 0, 1, 1, 2, 2)],
+            *[pltpu.VMEM((padded // LANES, 2 * lines // 2 ** i, LANES), f32) for i in (0, 0, 1, 1, 2, 2)],
             sem((3,)), sem((3,)), sem((3, 2)), sem((3, 2)),
             pltpu.VMEM((padded, pixels), f32), pltpu.VMEM((1, padded), f32),
             pltpu.VMEM((devices - 1, 1, padded), f32), pltpu.VMEM((total, LANES), f32),

time: 73.1 us -> 66.3 us (0.907)
  Pallas kernels: 68 us -> 61.2 us
    pallas_call x1, Pallas kernels: 68 us -> 61.2 us  [gram_call(): pl.pallas_call(functools.partial(gram_kernel, samp, line, bands, lines, w...]
where the time goes in v3:
time: 66.3 us; the launch traced here: 66 us
  Pallas kernels  61.2 us (92%)
  local copies, waits for them, and re-layouts  4.12 us (6%)
    pallas_call x1, Pallas kernels, gram_call(): pl.pallas_call(functools.partial(gram_kernel, samp, line, bands, lines, w...  61.2 us
    unnamed x10, local copies, waits for them, and re-layouts  4.12 us

profile of v3, /device:TPU:0, one launch (start us, length us, event | category | flops | bytes accessed | tf_op | source)
XLA Modules:
  0.0 66.0 jit_solution(4014179270629386896)
XLA Ops:
  0.6 61.2 %shard_map.46 = (f32[3,432,128]{2,1,0:T(8,128)}, f32[324,128]{1,0:T(8,128)}, f32[81,128]{1,0:T(8,128)}, f32[27,128]{1,0:T(8,128)}) custom-call(f32[1728,128]{1,0:T(8,128)} %bitcast.5), custom_call_target="tpu_custom_call" | custom-call | tf_op jit(solution)/shard_map/pallas_call | solution.py:405
  61.8 0.0 copy-start
  61.9 2.0 %copy.9 = f32[165888]{0:T(1024)} copy(f32[165888]{0:T(1024)} %bitcast.6) | data formatting | bytes 1327104
  63.9 0.0 copy-done
  63.9 0.0 copy-start.1
  63.9 0.7 %copy.10 = f32[41472]{0:T(1024)} copy(f32[41472]{0:T(1024)S(1)} %bitcast.7) | data formatting | bytes 331776
  64.6 0.1 copy-done.1
  64.7 0.0 copy-start.2
  64.7 0.6 copy.11
  65.3 0.1 copy-done.2
  65.4 0.6 copy.12
Async XLA Ops:
  61.8 2.0 %copy-start = (f32[324,128]{1,0:T(8,128)S(1)}, f32[324,128]{1,0:T(8,128)}, u32[]{:S(2)}) copy-start(f32[324,128]{1,0:T(8,128)} %get-tuple-element.9) | copy-start | bytes 497668
  63.9 0.8 %copy-start.1 = (f32[81,128]{1,0:T(8,128)S(1)}, f32[81,128]{1,0:T(8,128)}, u32[]{:S(2)}) copy-start(f32[81,128]{1,0:T(8,128)} %get-tuple-element.10) | copy-start | bytes 124420
  64.7 0.7 %copy-start.2 = (f32[27,128]{1,0:T(8,128)S(1)}, f32[27,128]{1,0:T(8,128)}, u32[]{:S(2)}) copy-start(f32[27,128]{1,0:T(8,128)} %get-tuple-element.11) | copy-start | bytes 41476

commit v4 on v3

--- a/solution.py
+++ b/solution.py
@@ -274,7 +274,7 @@
         top = c * LANES
         span = bands - top
 
-        def step(j, carry):
+        def step(skip, j, carry):
             row = pl.multiple_of(top + 8 * j, 8)
             here = m[pl.ds(row, 8), top:top + LANES]
             small = pltpu.roll(here, lax.rem(LANES - 8 * j, LANES), 1)
@@ -328,16 +328,20 @@
                 (((0,), (0,)), ((), ())), preferred_element_type=jnp.float32)
             for t in range(wide // LANES):
                 part = slice(t * LANES, (t + 1) * LANES)
-                old = m[top:bands, part]
+                old = m[top + skip:bands, part]
                 if t == c:
-                    line_ids = lax.broadcasted_iota(jnp.int32, (span, LANES), 0)
-                    lane_ids = lax.broadcasted_iota(jnp.int32, (span, LANES), 1)
+                    line_ids = lax.broadcasted_iota(jnp.int32, (span - skip, LANES), 0) + skip
+                    lane_ids = lax.broadcasted_iota(jnp.int32, (span - skip, LANES), 1)
                     inside = (lane_ids >= 8 * j) & (lane_ids < 8 * j + 8) & (line_ids >= 8 * j + 8)
                     old = jnp.where(inside, 0.0, old)
-                m[top:bands, part] = old - update[:span, part]
+                m[top + skip:bands, part] = old - update[skip:span, part]
             return carry
 
-        lax.fori_loop(0, min(LANES, span) // 8, step, 0)
+        steps = min(LANES, span) // 8
+        middle = min(8, steps)
+        lax.fori_loop(0, middle, functools.partial(step, 0), 0)
+        if steps > middle:
+            lax.fori_loop(middle, steps, functools.partial(step, 8 * middle), 0)
     eliminate(0)
     rim_wait(pair)
     h, w = lines // 2, width // 2

time: 66.3 us -> 66.3 us (level)
  no operation moved by 1% of the time
where the time goes in v4:
time: 66.3 us; the launch traced here: 66 us
  Pallas kernels  61.2 us (92%)
  local copies, waits for them, and re-layouts  4.12 us (6%)
    pallas_call x1, Pallas kernels, gram_call(): pl.pallas_call(functools.partial(gram_kernel, samp, line, bands, lines, w...  61.2 us
    unnamed x10, local copies, waits for them, and re-layouts  4.12 us

profile of v4, /device:TPU:0, one launch (start us, length us, event | category | flops | bytes accessed | tf_op | source)
XLA Modules:
  0.0 66.0 jit_solution(11100426462837863076)
XLA Ops:
  0.6 61.2 %shard_map.46 = (f32[3,432,128]{2,1,0:T(8,128)}, f32[324,128]{1,0:T(8,128)}, f32[81,128]{1,0:T(8,128)}, f32[27,128]{1,0:T(8,128)}) custom-call(f32[1728,128]{1,0:T(8,128)} %bitcast.5), custom_call_target="tpu_custom_call" | custom-call | tf_op jit(solution)/shard_map/pallas_call | solution.py:409
  61.8 0.0 copy-start
  61.9 2.0 %copy.9 = f32[165888]{0:T(1024)} copy(f32[165888]{0:T(1024)} %bitcast.6) | data formatting | bytes 1327104
  63.9 0.0 copy-done
  63.9 0.0 copy-start.1
  63.9 0.7 %copy.10 = f32[41472]{0:T(1024)} copy(f32[41472]{0:T(1024)S(1)} %bitcast.7) | data formatting | bytes 331776
  64.6 0.1 copy-done.1
  64.7 0.0 copy-start.2
  64.7 0.6 copy.11
  65.3 0.1 copy-done.2
  65.4 0.6 copy.12
Async XLA Ops:
  61.8 2.0 %copy-start = (f32[324,128]{1,0:T(8,128)S(1)}, f32[324,128]{1,0:T(8,128)}, u32[]{:S(2)}) copy-start(f32[324,128]{1,0:T(8,128)} %get-tuple-element.9) | copy-start | bytes 497668
  63.9 0.8 %copy-start.1 = (f32[81,128]{1,0:T(8,128)S(1)}, f32[81,128]{1,0:T(8,128)}, u32[]{:S(2)}) copy-start(f32[81,128]{1,0:T(8,128)} %get-tuple-element.10) | copy-start | bytes 124420
  64.7 0.7 %copy-start.2 = (f32[27,128]{1,0:T(8,128)S(1)}, f32[27,128]{1,0:T(8,128)}, u32[]{:S(2)}) copy-start(f32[27,128]{1,0:T(8,128)} %get-tuple-element.11) | copy-start | bytes 41476
